TPU v7x, 32 devices: a whole 2x2x4 slice. The times are simulated.
32 devices in a mesh: groups: 2 (over x), ctx: 4 (over y, core), heads: 4 (over z).
Axes of the slice: x: 2, y: 2, z: 4, core: 2. Of those that a mesh axis runs over, the one named last changes fastest.
Arguments:
- tokens: bfloat16 [4096, 2048], P(('groups', 'ctx', 'heads')), parts along dimension 0, may hold values from -60 to 60
- state_in: float32 [4, 256, 128], P('heads', 'groups'), parts along dimension 1, may hold values from -256 to 256
- past_kv: bfloat16 [2, 1024, 512], P(None, 'groups', 'heads'), parts along dimension 1, may hold values from -6 to 6
- w_qkv: bfloat16 [2048, 3, 512], P(None, None, 'heads'), may hold values from -0.125 to 0.125
- w_out: bfloat16 [512, 2048], P('heads'), may hold values from -0.25 to 0.25
- w_gate: bfloat16 [16, 2048, 768], P(('ctx', 'heads')), may hold values from -0.125 to 0.125
- w_up: bfloat16 [16, 2048, 768], P(('ctx', 'heads')), may hold values from -0.125 to 0.125
- w_down: bfloat16 [16, 768, 2048], P(('ctx', 'heads')), may hold values from -0.21875 to 0.21875
- expert_ids: int32 [4096, 8], P(('groups', 'ctx', 'heads')), parts along dimension 0, may hold values from 0 to 15, all different within a row; in each aligned block of 128 rows (0 to 127, 128 to 255, ...) at most 128 rows name the same one
- gate_weights: float32 [4096, 8], P(('groups', 'ctx', 'heads')), parts along dimension 0, may hold values from 0.1 to 1
Outputs:
- mixed: bfloat16 [4096, 2048], P(('groups', 'ctx', 'heads')), parts along dimension 0
There are 2 independent parts, one for each index of `groups`. A program takes and returns all parts, laid end to end along the dimension named above; an argument that names none is the same for every part. Nothing has to cross between parts.
Inputs may be any that keep to these rules, and one draw needn't show every extreme that they name: `expert_ids`: each row names 8 different experts; in each aligned block of 128 rows (the rows of one device) no expert is named by more than 128 rows, a bound that some block reaches.
All inputs are finite; a program needn't handle non-finite values.
Results may differ from a plain program's by a relative error of at most 0.017.
Values may be sent and summed in bfloat16 or wider, within the bound.
A program may use at most 128 MiB of HBM per device.

v0:
```python
import math

import jax
import jax.numpy as jnp
from jax import lax
from jax.sharding import PartitionSpec as P

HDIM = 128
WINDOW = 512


def entering(x, axis, join, neutral):
    place = lax.axis_index(axis)
    gathered = lax.all_gather(x.astype(jnp.bfloat16), axis)
    state = jnp.zeros_like(x) + jnp.asarray(neutral, x.dtype)

    def one(lap, state):
        return join(state, lax.dynamic_index_in_dim(gathered, lap, 0, False).astype(x.dtype))

    return lax.fori_loop(0, place, one, state)


def from_behind(block, axis, distance):
    devices = range(lax.axis_size(axis))
    route = [(i - distance, i) for i in devices if i - distance in devices]
    return lax.ppermute(block, axis, route)


def normalize(value):
    return value * lax.rsqrt(jnp.mean(value * value, axis=-1, keepdims=True) + 1e-06)


def on_device(
    tokens, state_in, past_kv, w_qkv, w_out, w_gate, w_up, w_down, expert_ids, gate_weights
):
    row_count, model_width = tokens.shape
    inner_width = w_qkv.shape[2]
    local_heads = inner_width // HDIM
    w_flat = w_qkv.reshape(model_width, 3 * inner_width)
    projected = jnp.dot(
        lax.all_gather(tokens, "heads", axis=0, tiled=True),
        w_flat,
        preferred_element_type=jnp.float32,
    ).astype(jnp.bfloat16)
    slab_rows = projected.shape[0]
    projected = projected.reshape(slab_rows, 3, local_heads, HDIM)
    query = jnp.transpose(projected[:, 0], (1, 0, 2))
    keys = jnp.transpose(projected[:, 1], (1, 0, 2))
    values = jnp.transpose(projected[:, 2], (1, 0, 2))
    local_state = jnp.einsum("hsd,hse->hde", keys, values, preferred_element_type=jnp.float32)
    earlier_state = entering(
        local_state, "ctx", lambda first, second: first + second, jnp.zeros_like(local_state)
    )
    start_state = state_in + earlier_state
    tail = jnp.stack([keys, values], axis=0)
    arrived = from_behind(tail, "ctx", 1)
    past = jnp.transpose(past_kv.reshape(2, WINDOW, local_heads, HDIM), (0, 2, 1, 3))
    previous = jnp.where(lax.axis_index("ctx") == 0, past, arrived)
    all_keys = jnp.concatenate([previous[0], keys], axis=1)
    all_values = jnp.concatenate([previous[1], values], axis=1)
    block_rows = min(slab_rows, 512)
    block_count = slab_rows // block_rows
    scale = 1.0 / math.sqrt(HDIM)
    causal = jnp.arange(block_rows)[:, None] >= jnp.arange(block_rows)[None, :]
    offsets = jnp.arange(WINDOW + block_rows)[None, :] - jnp.arange(block_rows)[:, None]
    in_window = (offsets > 0) & (offsets <= WINDOW)

    def block_step(state, index):
        first = index * block_rows
        carried = jnp.einsum(
            "hsd,hde->hse", query.astype(jnp.float32), state, precision=lax.Precision.HIGHEST
        )
        inside = jnp.einsum("hsd,htd->hst", query, keys, preferred_element_type=jnp.float32)
        inside = jnp.where(causal[None], inside, 0.0).astype(jnp.bfloat16)
        linear = carried + jnp.einsum(
            "hst,hte->hse", inside, values, preferred_element_type=jnp.float32
        )
        scores = (
            jnp.einsum("hsd,htd->hst", query, all_keys, preferred_element_type=jnp.float32) * scale
        )
        scores = jnp.where(in_window[None], scores, -jnp.inf)
        top_score = jnp.max(scores, axis=-1, keepdims=True)
        expo = jnp.exp(scores - top_score)
        probs = (expo / jnp.sum(expo, axis=-1, keepdims=True)).astype(jnp.bfloat16)
        window_out = jnp.einsum(
            "hst,hte->hse", probs, all_values, preferred_element_type=jnp.float32
        )
        combined = (normalize(linear) + window_out).astype(jnp.bfloat16)
        new_state = state + jnp.einsum(
            "hsd,hse->hde", keys, values, preferred_element_type=jnp.float32
        )
        return (new_state, combined)

    _, outs = lax.scan(block_step, start_state, jnp.arange(block_count, dtype=jnp.int32))
    heads_out = jnp.transpose(outs, (0, 2, 1, 3)).reshape(slab_rows, inner_width)
    regrouped = lax.all_to_all(heads_out, "heads", split_axis=0, concat_axis=1, tiled=True)
    attn = jnp.dot(
        regrouped,
        lax.all_gather(w_out, "heads", axis=0, tiled=True),
        preferred_element_type=jnp.float32,
    )
    hidden_state = (tokens.astype(jnp.float32) + attn).astype(jnp.bfloat16)
    hidden_float = hidden_state.astype(jnp.float32)
    normed = normalize(hidden_float).astype(jnp.bfloat16)
    ctx_count = lax.axis_size("ctx")
    head_count = lax.axis_size("heads")
    exp_local = w_gate.shape[0]
    expert_count = exp_local * ctx_count * head_count
    top_count = expert_ids.shape[1]
    capacity = max(2, 2 * row_count * top_count // expert_count)
    picks = expert_ids.reshape(-1)
    onehot = (picks[:, None] == jnp.arange(expert_count, dtype=jnp.int32)[None, :]).astype(
        jnp.int32
    )
    earlier = jnp.cumsum(onehot, axis=0) - onehot
    slots = jnp.sum(onehot * earlier, axis=1)
    destination = picks * capacity + slots
    source_rows = jnp.arange(row_count * top_count, dtype=jnp.int32) // top_count
    outgoing = jnp.zeros((expert_count * capacity, model_width), jnp.bfloat16)
    outgoing = outgoing.at[destination].set(normed[source_rows])
    sendable = outgoing.reshape(expert_count, 1, capacity, model_width)
    arrived_rows = lax.all_to_all(
        sendable, ("ctx", "heads"), split_axis=0, concat_axis=1, tiled=True
    )
    e_count, n_count, c_count, d_count = arrived_rows.shape
    flat = arrived_rows.reshape(e_count, n_count * c_count, d_count)
    gate_act = jnp.einsum("erd,edf->erf", flat, w_gate, preferred_element_type=jnp.float32)
    up_act = jnp.einsum("erd,edf->erf", flat, w_up, preferred_element_type=jnp.float32)
    hid = (jax.nn.silu(gate_act) * up_act).astype(jnp.bfloat16)
    out_rows = jnp.einsum("erf,efd->erd", hid, w_down, preferred_element_type=jnp.float32)
    finished = out_rows.astype(jnp.bfloat16).reshape(e_count, n_count, c_count, d_count)
    returned = lax.all_to_all(finished, ("ctx", "heads"), split_axis=1, concat_axis=0, tiled=True)
    returned = returned.reshape(expert_count * capacity, model_width)
    picked = returned[destination].reshape(row_count, top_count, model_width).astype(jnp.float32)
    routed = jnp.sum(gate_weights[:, :, None] * picked, axis=1)
    return (hidden_float + routed).astype(jnp.bfloat16)


def solution(mesh):
    return jax.shard_map(
        on_device,
        mesh=mesh,
        in_specs=(
            P(("groups", "ctx", "heads"), None),
            P("heads", "groups", None),
            P(None, "groups", "heads"),
            P(None, None, "heads"),
            P("heads", None),
            P(("ctx", "heads"), None, None),
            P(("ctx", "heads"), None, None),
            P(("ctx", "heads"), None, None),
            P(("groups", "ctx", "heads"), None),
            P(("groups", "ctx", "heads"), None),
        ),
        out_specs=P(("groups", "ctx", "heads"), None),
        check_vma=False,
    )
```

profile of v0, /device:TPU:0, one launch (start us, length us, event | category | flops | bytes accessed | tf_op | source)
XLA Modules:
  0.0 573.4 jit_solution(15762192888532435691)
XLA Ops:
  6.5 0.7 all-gather.4.cloned.1.call-update
  8.0 0.8 copy.41
  9.7 2.6 copy.32
  12.3 4.5 reduce-window.6
  17.5 39.8 %all-gather.4.cloned.1.call-done = bf16[512,2048]{1,0:T(8,128)(2,1)} async-done(((bf16[128,2048]{1,0:T(8,128)(2,1)}), bf16[512,2048]{1,0:T(8,128)(2,1)}) %all-gather.4.cloned.1.call-update) | async-done | bytes 2097168 | tf_op jit(solution)/shard_map/all_gather | solution.py:41
  57.3 3.1 convolution_convert_fusion.1
  60.4 0.7 fusion.46
  61.2 0.8 convolution_convert_fusion.2
  62.1 1.1 copy.47
  63.2 0.8 pad_maximum_fusion
  63.9 2.3 collective-permute-start
  66.2 6.0 %all-gather = bf16[512,128]{1,0:T(8,128)(2,1)S(1)} all-gather(bf16[128,128]{1,0:T(8,128)(2,1)} %convolution_convert_fusion.2), channel_id=2, replica_groups=mesh['groups'=2,'ctx'=4,'heads'=4] {'ctx'}, dimensions={0}, use_global_device_ids=true | all-gather | bytes 163840 | tf_op jit(solution)/shard_map/all_gather | solution.py:14
  72.3 2.0 fusion.30
  74.2 2.3 multiply_reduce_fusion.1
  76.6 1.1 bitcast_select_fusion
  77.7 1.5 fusion.47
  80.3 0.8 copy.38
  81.1 3.5 all-to-all-start
  84.6 21.6 %all-gather.6.cloned.1.call-done = bf16[512,2048]{1,0:T(8,128)(2,1)} async-done(((bf16[128,2048]{1,0:T(8,128)(2,1)}), bf16[512,2048]{1,0:T(8,128)(2,1)}) %all-gather.6.cloned.1.call-update) | async-done | bytes 2097168 | tf_op jit(solution)/shard_map/all_gather | solution.py:99
  106.2 2.2 multiply_reduce_fusion
  108.5 1.0 copy-done.2
  109.4 0.9 multiply_convert_fusion.1
  110.4 24.7 %scatter_custom_fusion = bf16[2048,2048]{1,0:T(8,128)(2,1)} fusion(s32[1024]{0:T(1024)S(1)} %bitcast.134, bf16[128,2048]{1,0:T(8,128)(2,1)} %multiply_convert_fusion.1, s32[1024]{0:T(1024)S(1)} %broadcast_clamp_fusion.1, bf16[]{:T(256)} %constant.69.clone.1), kind=kCustom, calls=%fused_computation.8 | custom fusion | bytes 8389120 | tf_op jit(solution)/shard_map/scatter | solution.py:120
  135.1 188.4 %all_to_all.37 = bf16[16,1,128,2048]{3,2,1,0:T(8,128)(2,1)S(1)} all-to-all(bf16[16,1,128,2048]{3,2,1,0:T(8,128)(2,1)} %bitcast.113), channel_id=1, replica_groups=mesh['groups'=2,'ctx'=4,'heads'=4] {'ctx','heads'}, dimensions={0} | all-to-all | bytes 16777216 | tf_op jit(solution)/shard_map/all_to_all | solution.py:122
  323.5 3.2 copy-done.4
  326.7 8.5 %fusion.7 = f32[2048,768]{1,0:T(8,128)} fusion(bf16[2048,2048]{1,0:T(8,128)(2,1)S(1)} %bitcast.115, bf16[1,2048,768]{2,1,0:T(8,128)(2,1)S(1)} %copy-done.10), kind=kOutput, calls=%fused_computation.13 | convolution fusion | flops 6442450944 | bytes 17825792 | tf_op jit(solution)/shard_map/erd,edf->erf/dot_general | solution.py:127
  335.2 21.3 %convolution_convert_fusion = bf16[2048,2048]{1,0:T(8,128)(2,1)} fusion(f32[2048,768]{1,0:T(8,128)} %fusion.7, bf16[2048,2048]{1,0:T(8,128)(2,1)} %bitcast.116, bf16[1,768,2048]{2,1,0:T(8,128)(2,1)S(1)} %copy-done, bf16[1,2048,768]{2,1,0:T(8,128)(2,1)} %param.18), kind=kOutput, calls=%fused_computation.6 | convolution fusion | flops 12898533376 | bytes 29360128 | tf_op jit(solution)/shard_map/erf,efd->erd/dot_general | solution.py:130
  356.5 5.2 all-to-all-start.2
  361.8 183.8 %all-to-all-done.2 = bf16[1,16,128,2048]{3,2,0,1:T(8,128)(2,1)} async-done(((bf16[1,16,128,2048]{3,2,0,1:T(8,128)(2,1)}), bf16[1,16,128,2048]{3,2,0,1:T(8,128)(2,1)}, u32[]{:S(2)}, u32[]{:S(2)}) %all-to-all-start.2) | async-done | bytes 8388640 | tf_op jit(solution)/shard_map/all_to_all | solution.py:132
  545.6 13.4 %gather_fusion = bf16[1024,2048]{1,0:T(8,128)(2,1)} fusion(bf16[2048,2048]{1,0:T(8,128)(2,1)} %bitcast.35, s32[1024]{0:T(1024)S(1)} %broadcast_clamp_fusion), kind=kCustom, calls=%fused_computation.1 | custom fusion | bytes 8392704 | tf_op jit(solution)/shard_map/gather | solution.py:134
  559.1 6.6 %fusion = f32[128,2048]{1,0:T(8,128)S(1)} fusion(bf16[1024,2048]{1,0:T(8,128)(2,1)} %gather_fusion, f32[128,8]{1,0:T(8,128)S(1)} %copy.39), kind=kLoop, calls=%fused_computation.5 | loop fusion | flops 6029312 | bytes 5246976 | tf_op jit(solution)/shard_map/reduce_sum | solution.py:135
  565.7 0.9 add_convert_fusion
  (54 shorter events, 3.7 us)
Async XLA Ops:
  6.5 328.7 %copy-start = (bf16[1,768,2048]{2,1,0:T(8,128)(2,1)S(1)}, bf16[1,768,2048]{2,1,0:T(8,128)(2,1)}, u32[]{:S(2)}) copy-start(bf16[1,768,2048]{2,1,0:T(8,128)(2,1)} %param.19) | copy-start | bytes 9437188
  6.5 50.8 %all-gather.4.cloned.1.call-start = ((), (), s32[]{:S(2)}) async-start(), calls=%async_computation.3 | async-start | bytes 2621440 | tf_op jit(solution)/shard_map/all_gather | solution.py:41
  7.3 99.0 %all-gather.6.cloned.1.call-start = ((), (), s32[]{:S(2)}) async-start(), calls=%async_computation.4 | async-start | bytes 2621440 | tf_op jit(solution)/shard_map/all_gather | solution.py:99
  57.3 14.9 %copy-start.8 = (f32[1,128,128]{2,1,0:T(8,128)S(1)}, f32[1,128,128]{2,1,0:T(8,128)}, u32[]{:S(2)}) copy-start(f32[1,128,128]{2,1,0:T(8,128)} %param.13) | copy-start | bytes 196612
  60.4 1.5 copy-start.7
  62.1 1.8 copy-start.5
  63.9 12.6 %collective-permute-start = (bf16[2,1,512,128]{3,2,1,0:T(8,128)(2,1)}, bf16[2,1,512,128]{3,2,1,0:T(8,128)(2,1)}, u32[]{:S(2)}, u32[]{:S(2)}) collective-permute-start(bf16[2,1,512,128]{3,2,1,0:T(8,128)(2,1)} %pad_maximum_fusion), channel_id=1, source_target_pairs={{0,4},{4,8},{8,12},{1,5},{5,9},{9,13},{2,6},{6,10},{10,14},{3,7},{... | collective-permute-start | bytes 786440 | tf_op jit(solution)/shard_map/ppermute | solution.py:26
  72.2 5.4 copy-start.6
  77.7 2.0 copy-start.11
  81.1 25.2 %all-to-all-start = ((bf16[4,128,128]{1,2,0:T(8,128)(2,1)}), bf16[4,128,128]{1,2,0:T(8,128)(2,1)S(1)}, u32[]{:S(2)}, u32[]{:S(2)}) async-start(bf16[4,128,128]{1,2,0:T(8,128)(2,1)} %copy.38), calls=%async_computation | async-start | bytes 262144 | tf_op jit(solution)/shard_map/all_to_all | solution.py:96
  108.4 1.0 copy-start.2
  135.1 191.6 %copy-start.10 = (bf16[1,2048,768]{2,1,0:T(8,128)(2,1)S(1)}, bf16[1,2048,768]{2,1,0:T(8,128)(2,1)}, u32[]{:S(2)}) copy-start(bf16[1,2048,768]{2,1,0:T(8,128)(2,1)} %param.17) | copy-start | bytes 9437188
  323.5 3.2 copy-start.4
  356.5 5.2 copy-start.9
  356.5 189.1 %all-to-all-start.2 = ((bf16[1,16,128,2048]{3,2,0,1:T(8,128)(2,1)}), bf16[1,16,128,2048]{3,2,0,1:T(8,128)(2,1)}, u32[]{:S(2)}, u32[]{:S(2)}) async-start(bf16[1,16,128,2048]{3,2,0,1:T(8,128)(2,1)} %bitcast.114), calls=%async_computation.2 | async-start | bytes 16777216 | tf_op jit(solution)/shard_map/all_to_all | solution.py:132
  545.6 21.0 %copy-start.1 = (bf16[1,768,2048]{2,1,0:T(8,128)(2,1)S(1)}, bf16[1,768,2048]{2,1,0:T(8,128)(2,1)}, u32[]{:S(2)}) copy-start(bf16[1,768,2048]{2,1,0:T(8,128)(2,1)} %param.19) | copy-start | bytes 9437188
  559.0 6.6 %copy-start.3 = (f32[128,2048]{1,0:T(8,128)S(1)}, f32[128,2048]{1,0:T(8,128)}, u32[]{:S(2)}) copy-start(f32[128,2048]{1,0:T(8,128)} %copy-done.2) | copy-start | bytes 3145732
Sparse Core Ops, SparseCore 0:
  8.9 48.3 all-gather.3
  58.9 47.2 all-gather.5
where the time goes:
time: 574 us; the launch traced here: 573 us
  waiting for transfers between devices  247 us (43%)
  blocking collectives  194 us (34%)
  local copies, waits for them, and re-layouts  49.3 us (9%)
  matrix products  42.2 us (7%)
  other arithmetic  16.2 us (3%)
  between operations  13.6 us (2%)
  starting transfers between devices  11 us (2%)
    all_to_all x1, blocking collectives, on_device(): lax.all_to_all(sendable, ('ctx', 'heads'), split_axis=0, concat_axis=1, t...  188 us
    all_to_all x1, waiting for transfers between devices, on_device(): lax.all_to_all(finished, ('ctx', 'heads'), split_axis=1, concat_axis=0, t...  184 us
    all_gather x1, waiting for transfers between devices, on_device(): lax.all_gather(tokens, 'heads', axis=0, tiled=True)  39.8 us
    scatter x1, local copies, waits for them, and re-layouts, on_device(): outgoing = outgoing.at[destination].set(normed[source_rows])  24.7 us
    all_gather x1, waiting for transfers between devices, on_device(): lax.all_gather(w_out, 'heads', axis=0, tiled=True)  21.6 us
    dot_general x1, matrix products, on_device(): jnp.einsum('erf,efd->erd', hid, w_down, preferred_element_type=jnp.float32)  21.3 us
    gather x1, local copies, waits for them, and re-layouts, on_device(): returned[destination].reshape(row_count, top_count, model_width)  13.4 us
  transfers between devices with their start and end apart: 5, of which 3 were waited for; matrix products, arithmetic and copies ran while one was open for 4% of the time, Pallas kernels for 0%

commit v1 on v0

--- a/solution.py
+++ b/solution.py
@@ -28,6 +28,31 @@
 
 def normalize(value):
     return value * lax.rsqrt(jnp.mean(value * value, axis=-1, keepdims=True) + 1e-06)
+
+
+def dense_experts(
+    hidden_float, normed, w_gate, w_up, w_down, expert_ids, gate_weights, expert_count
+):
+    axes = ("ctx", "heads")
+    exp_local = w_gate.shape[0]
+    chosen = expert_ids[:, :, None] == jnp.arange(expert_count, dtype=jnp.int32)
+    table = jnp.sum(jnp.where(chosen, gate_weights[:, :, None], 0.0), axis=1)
+    weights = lax.all_gather(table, axes, axis=0, tiled=True)
+    first = lax.axis_index(axes) * exp_local
+    rows = lax.all_gather(normed, axes, axis=0, tiled=True)
+    total = None
+    for e in range(exp_local):
+        gate_act = jnp.dot(rows, w_gate[e], preferred_element_type=jnp.float32)
+        up_act = jnp.dot(rows, w_up[e], preferred_element_type=jnp.float32)
+        hid = (jax.nn.silu(gate_act) * up_act).astype(jnp.bfloat16)
+        out_rows = jnp.dot(hid, w_down[e], preferred_element_type=jnp.float32)
+        weight = lax.dynamic_slice_in_dim(weights, first + e, 1, 1)
+        part = weight * out_rows
+        total = part if total is None else total + part
+    routed = lax.psum_scatter(
+        total.astype(jnp.bfloat16), axes, scatter_dimension=0, tiled=True
+    )
+    return (hidden_float + routed.astype(jnp.float32)).astype(jnp.bfloat16)
 
 
 def on_device(
@@ -108,6 +133,11 @@
     expert_count = exp_local * ctx_count * head_count
     top_count = expert_ids.shape[1]
     capacity = max(2, 2 * row_count * top_count // expert_count)
+    devices = ctx_count * head_count
+    if row_count * devices <= expert_count * capacity:
+        return dense_experts(
+            hidden_float, normed, w_gate, w_up, w_down, expert_ids, gate_weights, expert_count
+        )
     picks = expert_ids.reshape(-1)
     onehot = (picks[:, None] == jnp.arange(expert_count, dtype=jnp.int32)[None, :]).astype(
         jnp.int32

time: 574 us -> 329 us (0.57)
  blocking collectives: 194 us -> 38.5 us
  local copies, waits for them, and re-layouts: 49.3 us -> 7.86 us
  waiting for transfers between devices: 247 us -> 212 us
  other arithmetic: 16.2 us -> 6.41 us
    all_to_all x1 -> x0, blocking collectives: 188 us -> none  [on_device(): lax.all_to_all(sendable, ('ctx', 'heads'), split_axis=0, concat_axis=1, t...]
    all_to_all x1 -> x0, waiting for transfers between devices: 184 us -> none  [on_device(): lax.all_to_all(finished, ('ctx', 'heads'), split_axis=1, concat_axis=0, t...]
    reduce_scatter x0 -> x1, waiting for transfers between devices: none -> 102 us  [dense_experts(): lax.psum_scatter(total.astype(jnp.bfloat16), axes, scatter_dimension=0, t...]
    all_gather x0 -> x1, waiting for transfers between devices: none -> 41.7 us  [dense_experts(): rows = lax.all_gather(normed, axes, axis=0, tiled=True)]
    all_gather x0 -> x1, blocking collectives: none -> 33.1 us  [dense_experts(): weights = lax.all_gather(table, axes, axis=0, tiled=True)]
    scatter x1 -> x0, local copies, waits for them, and re-layouts: 24.7 us -> none  [on_device(): outgoing = outgoing.at[destination].set(normed[source_rows])]
    gather x1 -> x0, local copies, waits for them, and re-layouts: 13.4 us -> none  [on_device(): returned[destination].reshape(row_count, top_count, model_width)]
    all_gather x1, waiting for transfers between devices: 39.8 us -> 46.7 us  [on_device(): lax.all_gather(tokens, 'heads', axis=0, tiled=True)]
  transfers between devices with their start and end apart: 5 -> 6, of which waited for: 3 -> 4; matrix products, arithmetic and copies ran while one was open for 4% -> 6% of each run, Pallas kernels for 0% -> 0%
where the time goes in v1:
time: 329 us
  waiting for transfers between devices  212 us (64%)
  matrix products  44.1 us (13%)
  blocking collectives  38.5 us (12%)
  between operations  13.3 us (4%)
  local copies, waits for them, and re-layouts  7.86 us (2%)
  starting transfers between devices  6.54 us (2%)
  other arithmetic  6.41 us (2%)
    reduce_scatter x1, waiting for transfers between devices, dense_experts(): lax.psum_scatter(total.astype(jnp.bfloat16), axes, scatter_dimension=0, t...  102 us
    all_gather x1, waiting for transfers between devices, on_device(): lax.all_gather(tokens, 'heads', axis=0, tiled=True)  46.7 us
    all_gather x1, waiting for transfers between devices, dense_experts(): rows = lax.all_gather(normed, axes, axis=0, tiled=True)  41.7 us
    all_gather x1, blocking collectives, dense_experts(): weights = lax.all_gather(table, axes, axis=0, tiled=True)  33.1 us
    dot_general x1, matrix products, dense_experts(): out_rows = jnp.dot(hid, w_down[e], preferred_element_type=jnp.float32)  20.6 us
    all_gather x1, waiting for transfers between devices, on_device(): lax.all_gather(w_out, 'heads', axis=0, tiled=True)  19.8 us
    dot_general x1, matrix products, dense_experts(): gate_act = jnp.dot(rows, w_gate[e], preferred_element_type=jnp.float32)  11.7 us
  transfers between devices with their start and end apart: 6, of which 4 were waited for; matrix products, arithmetic and copies ran while one was open for 6% of the time, Pallas kernels for 0%

profile of v1, /device:TPU:0, one launch (start us, length us, event | category | flops | bytes accessed | tf_op | source)
XLA Modules:
  0.0 328.5 jit_solution(8045174008604358506)
XLA Ops:
  6.5 0.7 all-gather.5.cloned.1.call-update
  7.3 0.7 all-gather.7.cloned.1.call-update
  8.0 2.6 copy.27
  10.6 46.7 %all-gather.5.cloned.1.call-done = bf16[512,2048]{1,0:T(8,128)(2,1)} async-done(((bf16[128,2048]{1,0:T(8,128)(2,1)}), bf16[512,2048]{1,0:T(8,128)(2,1)}) %all-gather.5.cloned.1.call-update) | async-done | bytes 2097168 | tf_op jit(solution)/shard_map/all_gather | solution.py:66
  57.3 3.1 convolution_convert_fusion
  60.4 0.2 convolution_convert_fusion.1
  60.6 0.7 fusion.38
  61.3 5.4 %all-gather = bf16[512,128]{1,0:T(8,128)(2,1)S(1)} all-gather(bf16[128,128]{1,0:T(8,128)(2,1)S(1)} %convolution_convert_fusion.1), channel_id=2, replica_groups=mesh['groups'=2,'ctx'=4,'heads'=4] {'ctx'}, dimensions={0}, use_global_device_ids=true | all-gather | bytes 163840 | tf_op jit(solution)/shard_map/all_gather | solution.py:14
  66.7 1.0 copy.35
  67.8 1.7 copy.34
  69.4 1.6 pad_maximum_fusion
  71.1 3.0 collective-permute-start
  74.0 2.0 fusion.26
  76.0 2.3 multiply_reduce_fusion.1
  78.3 1.1 bitcast_select_fusion
  79.4 1.5 fusion.39
  80.9 0.5 fusion.11
  81.5 0.6 fusion.15
  82.1 0.8 copy.33
  82.8 3.5 %all-to-all-start = ((bf16[4,128,128]{1,2,0:T(8,128)(2,1)}), bf16[4,128,128]{1,2,0:T(8,128)(2,1)S(1)}, u32[]{:S(2)}, u32[]{:S(2)}) async-start(bf16[4,128,128]{1,2,0:T(8,128)(2,1)} %copy.33), calls=%async_computation | async-start | bytes 262144 | tf_op jit(solution)/shard_map/all_to_all | solution.py:121
  86.3 0.0 all-gather.9.cloned.1.call-start
  86.3 19.8 %all-gather.7.cloned.1.call-done = bf16[512,2048]{1,0:T(8,128)(2,1)} async-done(((bf16[128,2048]{1,0:T(8,128)(2,1)}), bf16[512,2048]{1,0:T(8,128)(2,1)}) %all-gather.7.cloned.1.call-update) | async-done | bytes 2097168 | tf_op jit(solution)/shard_map/all_gather | solution.py:124
  106.2 2.2 multiply_reduce_fusion
  108.4 1.0 copy-done.1
  109.4 0.9 multiply_convert_fusion.2
  110.4 0.0 reduce-scatter.2.cloned.1.call-start
  110.5 33.1 %all_gather.22 = f32[2048,16]{0,1:T(8,128)S(1)} all-gather(f32[128,16]{0,1:T(8,128)S(1)} %select_reduce_fusion), channel_id=1, replica_groups=mesh['groups'=2,'ctx'=4,'heads'=4] {'ctx','heads'}, dimensions={0}, use_global_device_ids=true | all-gather | bytes 139264 | tf_op jit(solution)/shard_map/all_gather | solution.py:40
  143.6 41.7 %all-gather.9.cloned.1.call-done = bf16[2048,2048]{1,0:T(8,128)(2,1)} async-done(((bf16[128,2048]{1,0:T(8,128)(2,1)}), bf16[2048,2048]{1,0:T(8,128)(2,1)}) %all-gather.9.cloned.1.call-update) | async-done | bytes 8388624 | tf_op jit(solution)/shard_map/all_gather | solution.py:42
  185.3 11.7 %fusion.3 = f32[2048,768]{1,0:T(8,128)} fusion(bf16[2048,2048]{1,0:T(8,128)(2,1)} %all-gather.9.cloned.1.call-done, bf16[1,2048,768]{2,1,0:T(8,128)(2,1)} %param.17), kind=kOutput, calls=%fused_computation.5 | convolution fusion | flops 6442450944 | bytes 17825792 | tf_op jit(solution)/shard_map/dot_general | solution.py:45
  197.0 20.6 %multiply_convert_fusion = bf16[2048,2048]{1,0:T(8,128)(2,1)} fusion(f32[2048]{0:T(1024)S(1)} %bitcast.98, f32[2048,768]{1,0:T(8,128)} %fusion.3, bf16[2048,2048]{1,0:T(8,128)(2,1)} %all-gather.9.cloned.1.call-done, bf16[1,768,2048]{2,1,0:T(8,128)(2,1)S(1)} %copy-done, bf16[1,2048,768]{2,1,0:T(8,128)(2,1)} %param.18), kind=kOutput, calls=%fused_computation.1 | convolution fusion | flops 12902727680 | bytes 29368320 | tf_op jit(solution)/shard_map/dot_general | solution.py:48
  217.6 102.2 %reduce-scatter.2.cloned.1.call-done = bf16[128,2048]{1,0:T(8,128)(2,1)} async-done(((bf16[2048,2048]{1,0:T(8,128)(2,1)}), bf16[128,2048]{1,0:T(8,128)(2,1)}) %reduce-scatter.2.cloned.1.call-update) | async-done | bytes 524304 | tf_op jit(solution)/shard_map/reduce_scatter | solution.py:52
  319.7 2.3 add_convert_fusion
  (29 shorter events, 0.2 us)
Async XLA Ops:
  6.5 190.4 %copy-start = (bf16[1,768,2048]{2,1,0:T(8,128)(2,1)S(1)}, bf16[1,768,2048]{2,1,0:T(8,128)(2,1)}, u32[]{:S(2)}) copy-start(bf16[1,768,2048]{2,1,0:T(8,128)(2,1)} %param.19) | copy-start | bytes 9437188
  6.5 50.8 %all-gather.5.cloned.1.call-start = ((), (), s32[]{:S(2)}) async-start(), calls=%async_computation.2 | async-start | bytes 2621440 | tf_op jit(solution)/shard_map/all_gather | solution.py:66
  7.3 98.9 %all-gather.7.cloned.1.call-start = ((), (), s32[]{:S(2)}) async-start(), calls=%async_computation.3 | async-start | bytes 2621440 | tf_op jit(solution)/shard_map/all_gather | solution.py:124
  57.3 16.7 %copy-start.4 = (f32[1,128,128]{2,1,0:T(8,128)S(1)}, f32[1,128,128]{2,1,0:T(8,128)}, u32[]{:S(2)}) copy-start(f32[1,128,128]{2,1,0:T(8,128)} %param.13) | copy-start | bytes 196612
  60.4 6.3 %copy-start.3 = (bf16[512,384]{0,1:T(8,128)(2,1)}, bf16[512,384]{0,1:T(8,128)(2,1)S(1)}, u32[]{:S(2)}) copy-start(bf16[512,384]{0,1:T(8,128)(2,1)S(1)} %convolution_convert_fusion) | copy-start | bytes 1179652
  71.1 7.3 %collective-permute-start = (bf16[2,1,512,128]{3,2,1,0:T(8,128)(2,1)}, bf16[2,1,512,128]{3,2,1,0:T(8,128)(2,1)}, u32[]{:S(2)}, u32[]{:S(2)}) collective-permute-start(bf16[2,1,512,128]{3,2,1,0:T(8,128)(2,1)} %pad_maximum_fusion), channel_id=1, source_target_pairs={{0,4},{4,8},{8,12},{1,5},{5,9},{9,13},{2,6},{6,10},{10,14},{3,7},{... | collective-permute-start | bytes 786440 | tf_op jit(solution)/shard_map/ppermute | solution.py:26
  74.0 5.4 %copy-start.2 = (bf16[512,1,1,128]{3,0,2,1:T(8,128)(2,1)S(1)}, bf16[512,1,1,128]{3,0,2,1:T(8,128)(2,1)}, u32[]{:S(2)}) copy-start(bf16[512,1,1,128]{3,0,2,1:T(8,128)(2,1)} %copy.34) | copy-start | bytes 393220
  79.4 2.1 copy-start.7
  82.8 27.6 %copy-start.5 = (f32[128,8]{0,1:T(8,128)S(1)}, f32[128,8]{0,1:T(8,128)}, u32[]{:S(2)}) copy-start(f32[128,8]{0,1:T(8,128)} %param.21) | copy-start | bytes 12292
  82.8 27.6 %copy-start.6 = (s32[128,8]{0,1:T(8,128)S(1)}, s32[128,8]{0,1:T(8,128)}, u32[]{:S(2)}) copy-start(s32[128,8]{0,1:T(8,128)} %param.20) | copy-start | bytes 12292
  82.8 23.4 %all-to-all-start = ((bf16[4,128,128]{1,2,0:T(8,128)(2,1)}), bf16[4,128,128]{1,2,0:T(8,128)(2,1)S(1)}, u32[]{:S(2)}, u32[]{:S(2)}) async-start(bf16[4,128,128]{1,2,0:T(8,128)(2,1)} %copy.33), calls=%async_computation | async-start | bytes 262144 | tf_op jit(solution)/shard_map/all_to_all | solution.py:121
  86.3 99.0 %all-gather.9.cloned.1.call-start = ((), (), s32[]{:S(2)}) async-start(), calls=%async_computation.4 | async-start | bytes 8912896 | tf_op jit(solution)/shard_map/all_gather | solution.py:42
  108.4 1.0 copy-start.1
  110.4 209.4 %reduce-scatter.2.cloned.1.call-start = ((), (), s32[]{:S(2)}) async-start(), calls=%async_computation.5 | async-start | bytes 8912896 | tf_op jit(solution)/shard_map/reduce_scatter | solution.py:52
Sparse Core Ops, SparseCore 0:
  8.9 48.3 all-gather.4
  58.9 47.2 all-gather.6
  110.5 74.7 all-gather.8
  217.7 101.9 reduce-scatter.1

commit v2 on v1

--- a/solution.py
+++ b/solution.py
@@ -1,8 +1,11 @@
+import functools
 import math
 
 import jax
 import jax.numpy as jnp
 from jax import lax
+from jax.experimental import pallas as pl
+from jax.experimental.pallas import tpu as pltpu
 from jax.sharding import PartitionSpec as P
 
 HDIM = 128
@@ -28,6 +31,321 @@
 
 def normalize(value):
     return value * lax.rsqrt(jnp.mean(value * value, axis=-1, keepdims=True) + 1e-06)
+
+
+MESH = pl.DeviceIdType.MESH
+VMEM_BYTES = 60 * 1024 * 1024
+ADD_ROWS = 16
+
+
+def place(count):
+    z = lax.axis_index("heads")
+    c = lax.axis_index("ctx")
+    beside = c + 1 - 2 * lax.rem(c, 2)
+    across = lax.rem(c + 2, 4)
+    diagonal = lax.rem(beside + 2, 4)
+    return z, c, beside, across, diagonal
+
+
+def greet(z, count, beside, across):
+    barrier = pltpu.get_barrier_semaphore()
+
+    def signal(target):
+        pl.semaphore_signal(barrier, inc=1, device_id=target, device_id_type=MESH)
+
+    signal({"ctx": beside})
+    signal({"ctx": across})
+
+    @pl.when(z > 0)
+    def _():
+        signal({"heads": z - 1})
+
+    @pl.when(z < count - 1)
+    def _():
+        signal({"heads": z + 1})
+
+    pl.semaphore_wait(barrier, 2 + jnp.minimum(z, 1) + jnp.minimum(count - 1 - z, 1))
+
+
+def gather_kernel(
+    count, x_ref, t_ref, rows_ref, table_ref, send_x, send_t, recv_x, recv_t, own_sem
+):
+    z, c, beside, across, diagonal = place(count)
+    greet(z, count, beside, across)
+
+    def copies(zz, cc, way, target, own=False):
+        slot = cc * count + zz
+        return [
+            pltpu.make_async_remote_copy(
+                src_ref=source if own else full.at[slot],
+                dst_ref=full.at[slot],
+                send_sem=send.at[way, slot],
+                recv_sem=recv.at[slot],
+                device_id=target,
+                device_id_type=MESH,
+            )
+            for source, full, send, recv in (
+                (x_ref, rows_ref, send_x, recv_x),
+                (t_ref, table_ref, send_t, recv_t),
+            )
+        ]
+
+    def start(zz, cc, way, target, own=False):
+        for copy in copies(zz, cc, way, target, own):
+            copy.start()
+
+    def arrived(zz, cc):
+        for copy in copies(zz, cc, 0, {"ctx": beside}):
+            copy.wait_recv()
+
+    def left(zz, cc, way, target):
+        for copy in copies(zz, cc, way, target):
+            copy.wait_send()
+
+    def along(act, down, up, zz, **options):
+        if down:
+
+            @pl.when(z > 0)
+            def _():
+                act(zz, c, 0, {"heads": z - 1}, **options)
+
+        if up:
+
+            @pl.when(z < count - 1)
+            def _():
+                act(zz, c, 1, {"heads": z + 1}, **options)
+
+        act(zz, c, 2, {"ctx": across}, **options)
+        act(zz, c, 3, {"ctx": beside}, **options)
+
+    mine = c * count + z
+    local = [
+        pltpu.make_async_copy(x_ref, rows_ref.at[mine], own_sem.at[0]),
+        pltpu.make_async_copy(t_ref, table_ref.at[mine], own_sem.at[1]),
+    ]
+    for copy in local:
+        copy.start()
+    along(start, True, True, z, own=True)
+
+    def over(zz):
+        arrived(zz, across)
+        start(zz, across, 3, {"ctx": beside})
+
+    for d in range(1, count + 1):
+        if d < count:
+
+            @pl.when(z >= d)
+            def _():
+                arrived(z - d, c)
+                along(start, False, True, z - d)
+
+            @pl.when(z + d < count)
+            def _():
+                arrived(z + d, c)
+                along(start, True, False, z + d)
+
+        if d == 1:
+            over(z)
+        else:
+
+            @pl.when(z >= d - 1)
+            def _():
+                over(z - d + 1)
+
+            @pl.when(z + d - 1 < count)
+            def _():
+                over(z + d - 1)
+
+    for zz in range(count):
+        arrived(zz, beside)
+        arrived(zz, diagonal)
+    for copy in local:
+        copy.wait()
+    along(left, True, True, z)
+    for d in range(1, count):
+
+        @pl.when(z >= d)
+        def _():
+            along(left, False, True, z - d)
+
+        @pl.when(z + d < count)
+        def _():
+            along(left, True, False, z + d)
+
+    for zz in range(count):
+        left(zz, across, 3, {"ctx": beside})
+
+
+def scatter_kernel(
+    count, part_ref, out_ref, from_beside, from_across, below, above, to_across, to_line,
+    beside_send, beside_recv, across_send, across_recv, line_send, below_recv, above_recv,
+):
+    z, c, beside, across, diagonal = place(count)
+    greet(z, count, beside, across)
+
+    def by_distance(act):
+        for d in range(count - 1, 0, -1):
+
+            @pl.when(z + d < count)
+            def _():
+                act(z + d, 1)
+
+            @pl.when(z >= d)
+            def _():
+                act(z - d, -1)
+
+        act(z, 0)
+
+    def beside_copy(kind, zz):
+        cc = diagonal if kind == 0 else beside
+        return pltpu.make_async_remote_copy(
+            src_ref=part_ref.at[cc * count + zz],
+            dst_ref=from_beside.at[kind, zz],
+            send_sem=beside_send.at[kind, zz],
+            recv_sem=beside_recv.at[kind, zz],
+            device_id={"ctx": beside},
+            device_id_type=MESH,
+        )
+
+    def across_copy(zz):
+        return pltpu.make_async_remote_copy(
+            src_ref=to_across.at[zz],
+            dst_ref=from_across.at[zz],
+            send_sem=across_send.at[zz],
+            recv_sem=across_recv.at[zz],
+            device_id={"ctx": across},
+            device_id_type=MESH,
+        )
+
+    def up_copy(zz):
+        return pltpu.make_async_remote_copy(
+            src_ref=to_line.at[zz],
+            dst_ref=below.at[zz],
+            send_sem=line_send.at[zz],
+            recv_sem=below_recv.at[zz],
+            device_id={"heads": z + 1},
+            device_id_type=MESH,
+        )
+
+    def down_copy(zz):
+        return pltpu.make_async_remote_copy(
+            src_ref=to_line.at[zz],
+            dst_ref=above.at[zz],
+            send_sem=line_send.at[zz],
+            recv_sem=above_recv.at[zz],
+            device_id={"heads": z - 1},
+            device_id_type=MESH,
+        )
+
+    def add(target, sources):
+        def chunk(index, _):
+            rows = pl.ds(pl.multiple_of(index * ADD_ROWS, ADD_ROWS), ADD_ROWS)
+            total = sources[0][rows, :].astype(jnp.float32)
+            for source in sources[1:]:
+                total = total + source[rows, :].astype(jnp.float32)
+            target[rows, :] = total.astype(target.dtype)
+            return 0
+
+        lax.fori_loop(0, target.shape[0] // ADD_ROWS, chunk, 0)
+
+    by_distance(lambda zz, side: beside_copy(0, zz).start())
+    by_distance(lambda zz, side: beside_copy(1, zz).start())
+
+    def pass_across(zz, side):
+        beside_copy(0, zz).wait_recv()
+        add(to_across.at[zz], [part_ref.at[across * count + zz], from_beside.at[0, zz]])
+        across_copy(zz).start()
+
+    by_distance(pass_across)
+
+    def pass_line(zz, side):
+        beside_copy(1, zz).wait_recv()
+        across_copy(zz).wait_recv()
+        sources = [part_ref.at[c * count + zz], from_beside.at[1, zz], from_across.at[zz]]
+        if side == 0:
+            add(out_ref, sources)
+
+            @pl.when(z > 0)
+            def _():
+                up_copy(zz).wait_recv()
+                add(out_ref, [out_ref, below.at[zz]])
+
+            @pl.when(z < count - 1)
+            def _():
+                down_copy(zz).wait_recv()
+                add(out_ref, [out_ref, above.at[zz]])
+
+            return
+        first = z == 0 if side > 0 else z == count - 1
+        copy = up_copy if side > 0 else down_copy
+        arriving = below if side > 0 else above
+
+        @pl.when(first)
+        def _():
+            add(to_line.at[zz], sources)
+
+        @pl.when(jnp.logical_not(first))
+        def _():
+            copy(zz).wait_recv()
+            add(to_line.at[zz], sources + [arriving.at[zz]])
+
+        copy(zz).start()
+
+    by_distance(pass_line)
+
+    def sent(zz, side):
+        beside_copy(0, zz).wait_send()
+        beside_copy(1, zz).wait_send()
+        across_copy(zz).wait_send()
+        if side > 0:
+            up_copy(zz).wait_send()
+        if side < 0:
+            down_copy(zz).wait_send()
+
+    by_distance(sent)
+
+
+def gather_rows(normed, table):
+    count, devices = lax.axis_size("heads"), lax.axis_size("heads") * lax.axis_size("ctx")
+    return pl.pallas_call(
+        functools.partial(gather_kernel, count),
+        out_shape=[
+            jax.ShapeDtypeStruct((devices,) + value.shape, value.dtype)
+            for value in (normed, table)
+        ],
+        in_specs=[pl.BlockSpec(memory_space=pltpu.VMEM)] * 2,
+        out_specs=[pl.BlockSpec(memory_space=pl.ANY)] * 2,
+        scratch_shapes=[
+            pltpu.SemaphoreType.DMA((4, devices)),
+            pltpu.SemaphoreType.DMA((4, devices)),
+            pltpu.SemaphoreType.DMA((devices,)),
+            pltpu.SemaphoreType.DMA((devices,)),
+            pltpu.SemaphoreType.DMA((2,)),
+        ],
+        compiler_params=pltpu.CompilerParams(collective_id=0, has_side_effects=True),
+        name="gather_rows",
+    )(normed, table)
+
+
+def scatter_sums(parts):
+    count = lax.axis_size("heads")
+    _, rows, width = parts.shape
+    block = (rows, width)
+    dma = pltpu.SemaphoreType.DMA
+    return pl.pallas_call(
+        functools.partial(scatter_kernel, count),
+        out_shape=jax.ShapeDtypeStruct(block, jnp.float32),
+        in_specs=[pl.BlockSpec(memory_space=pltpu.VMEM)],
+        out_specs=pl.BlockSpec(memory_space=pltpu.VMEM),
+        scratch_shapes=[pltpu.VMEM((2, count) + block, parts.dtype)]
+        + [pltpu.VMEM((count,) + block, parts.dtype)] * 5
+        + [dma((2, count))] * 2
+        + [dma((count,))] * 5,
+        compiler_params=pltpu.CompilerParams(
+            collective_id=1, has_side_effects=True, vmem_limit_bytes=VMEM_BYTES
+        ),
+        name="scatter_sums",
+    )(parts)
 
 
 def dense_experts(
@@ -37,22 +355,22 @@
     exp_local = w_gate.shape[0]
     chosen = expert_ids[:, :, None] == jnp.arange(expert_count, dtype=jnp.int32)
     table = jnp.sum(jnp.where(chosen, gate_weights[:, :, None], 0.0), axis=1)
-    weights = lax.all_gather(table, axes, axis=0, tiled=True)
     first = lax.axis_index(axes) * exp_local
-    rows = lax.all_gather(normed, axes, axis=0, tiled=True)
+    rows, tables = gather_rows(normed, table.T)
+    device_count, row_count, width = rows.shape
+    rows = rows.reshape(device_count * row_count, width)
     total = None
     for e in range(exp_local):
         gate_act = jnp.dot(rows, w_gate[e], preferred_element_type=jnp.float32)
         up_act = jnp.dot(rows, w_up[e], preferred_element_type=jnp.float32)
         hid = (jax.nn.silu(gate_act) * up_act).astype(jnp.bfloat16)
         out_rows = jnp.dot(hid, w_down[e], preferred_element_type=jnp.float32)
-        weight = lax.dynamic_slice_in_dim(weights, first + e, 1, 1)
+        weight = lax.dynamic_slice_in_dim(tables, first + e, 1, 1).reshape(-1, 1)
         part = weight * out_rows
         total = part if total is None else total + part
-    routed = lax.psum_scatter(
-        total.astype(jnp.bfloat16), axes, scatter_dimension=0, tiled=True
-    )
-    return (hidden_float + routed.astype(jnp.float32)).astype(jnp.bfloat16)
+    parts = total.astype(jnp.bfloat16).reshape(device_count, row_count, width)
+    routed = scatter_sums(parts)
+    return (hidden_float + routed).astype(jnp.bfloat16)
 
 
 def on_device(
@@ -134,7 +452,7 @@
     top_count = expert_ids.shape[1]
     capacity = max(2, 2 * row_count * top_count // expert_count)
     devices = ctx_count * head_count
-    if row_count * devices <= expert_count * capacity:
+    if ctx_count == 4 and row_count * devices <= expert_count * capacity:
         return dense_experts(
             hidden_float, normed, w_gate, w_up, w_down, expert_ids, gate_weights, expert_count
         )

time: 329 us -> 267 us (0.81)
  waiting for transfers between devices: 212 us -> 67.4 us
  Pallas kernels: 0 us -> 114 us
  blocking collectives: 38.5 us -> 5.4 us
    pallas_call x0 -> x2, Pallas kernels: none -> 114 us  [the longest x1 58.5 us: scatter_sums(): pl.pallas_call(functools.partial(scatter_kernel, count), out_shape=jax.Sh...]
    reduce_scatter x1 -> x0, waiting for transfers between devices: 102 us -> none  [dense_experts(): lax.psum_scatter(total.astype(jnp.bfloat16), axes, scatter_dimension=0, t...]
    all_gather x1 -> x0, waiting for transfers between devices: 41.7 us -> none  [dense_experts(): rows = lax.all_gather(normed, axes, axis=0, tiled=True)]
    all_gather x1 -> x0, blocking collectives: 33.1 us -> none  [dense_experts(): weights = lax.all_gather(table, axes, axis=0, tiled=True)]
  transfers between devices with their start and end apart: 6 -> 4, of which waited for: 4 -> 2; matrix products, arithmetic and copies ran while one was open for 6% -> 8% of each run, Pallas kernels for 0% -> 0%
where the time goes in v2:
time: 267 us
  Pallas kernels  114 us (43%)
  waiting for transfers between devices  67.4 us (25%)
  matrix products  44.1 us (17%)
  between operations  13.6 us (5%)
  local copies, waits for them, and re-layouts  8.7 us (3%)
  other arithmetic  7.2 us (3%)
  starting transfers between devices  6.31 us (2%)
  blocking collectives  5.4 us (2%)
    pallas_call x1, Pallas kernels, scatter_sums(): pl.pallas_call(functools.partial(scatter_kernel, count), out_shape=jax.Sh...  58.5 us
    pallas_call x1, Pallas kernels, gather_rows(): pl.pallas_call(functools.partial(gather_kernel, count), out_shape=[jax.Sh...  55.5 us
    all_gather x1, waiting for transfers between devices, on_device(): lax.all_gather(tokens, 'heads', axis=0, tiled=True)  46.7 us
    dot_general x1, matrix products, dense_experts(): out_rows = jnp.dot(hid, w_down[e], preferred_element_type=jnp.float32)  20.6 us
    all_gather x1, waiting for transfers between devices, on_device(): lax.all_gather(w_out, 'heads', axis=0, tiled=True)  19.3 us
    dot_general x1, matrix products, dense_experts(): gate_act = jnp.dot(rows, w_gate[e], preferred_element_type=jnp.float32)  11.7 us
    unnamed x19, local copies, waits for them, and re-layouts  6.33 us
    all_gather x1, blocking collectives, entering(): gathered = lax.all_gather(x.astype(jnp.bfloat16), axis)  5.4 us
  transfers between devices with their start and end apart: 4, of which 2 were waited for; matrix products, arithmetic and copies ran while one was open for 8% of the time, Pallas kernels for 0%

profile of v2, /device:TPU:0, one launch (start us, length us, event | category | flops | bytes accessed | tf_op | source)
XLA Modules:
  0.0 266.8 jit_solution(981935929441647815)
XLA Ops:
  6.5 0.7 all-gather.4.cloned.1.call-update
  7.3 0.0 all-gather.6.cloned.1.call-start
  7.3 0.7 all-gather.6.cloned.1.call-update
  8.0 2.6 copy.27
  10.6 46.7 %all-gather.4.cloned.1.call-done = bf16[512,2048]{1,0:T(8,128)(2,1)} async-done(((bf16[128,2048]{1,0:T(8,128)(2,1)}), bf16[512,2048]{1,0:T(8,128)(2,1)}) %all-gather.4.cloned.1.call-update) | async-done | bytes 2097168 | tf_op jit(solution)/shard_map/all_gather | solution.py:384
  57.3 3.1 %convolution_convert_fusion = bf16[512,384]{0,1:T(8,128)(2,1)S(1)} fusion(bf16[512,2048]{1,0:T(8,128)(2,1)} %all-gather.4.cloned.1.call-done, bf16[2048,384]{0,1:T(8,128)(2,1)} %bitcast.88), kind=kOutput, calls=%fused_computation.21 | convolution fusion | flops 805502976 | bytes 4063232 | tf_op jit(solution)/shard_map/dot_general | solution.py:383
  60.4 0.2 convolution_convert_fusion.1
  60.6 0.7 fusion.38
  61.3 5.4 %all-gather = bf16[512,128]{1,0:T(8,128)(2,1)S(1)} all-gather(bf16[128,128]{1,0:T(8,128)(2,1)S(1)} %convolution_convert_fusion.1), channel_id=2, replica_groups=mesh['groups'=2,'ctx'=4,'heads'=4] {'ctx'}, dimensions={0}, use_global_device_ids=true | all-gather | bytes 163840 | tf_op jit(solution)/shard_map/all_gather | solution.py:17
  66.7 1.0 copy.35
  67.8 1.7 copy.34
  69.4 1.6 pad_maximum_fusion
  71.1 2.9 %collective-permute-start = (bf16[2,1,512,128]{3,2,1,0:T(8,128)(2,1)}, bf16[2,1,512,128]{3,2,1,0:T(8,128)(2,1)}, u32[]{:S(2)}, u32[]{:S(2)}) collective-permute-start(bf16[2,1,512,128]{3,2,1,0:T(8,128)(2,1)} %pad_maximum_fusion), channel_id=1, source_target_pairs={{0,4},{4,8},{8,12},{1,5},{5,9},{9,13},{2,6},{6,10},{10,14},{3,7},{... | collective-permute-start | bytes 786440 | tf_op jit(solution)/shard_map/ppermute | solution.py:29
  74.0 2.0 fusion.26
  76.0 2.3 multiply_reduce_fusion.1
  78.3 1.1 bitcast_select_fusion
  79.4 1.5 fusion.39
  81.0 0.5 fusion.11
  81.5 0.6 fusion.15
  82.1 0.8 copy.33
  82.9 3.3 %all-to-all-start = ((bf16[4,128,128]{1,2,0:T(8,128)(2,1)}), bf16[4,128,128]{1,2,0:T(8,128)(2,1)S(1)}, u32[]{:S(2)}, u32[]{:S(2)}) async-start(bf16[4,128,128]{1,2,0:T(8,128)(2,1)} %copy.33), calls=%async_computation | async-start | bytes 262144 | tf_op jit(solution)/shard_map/all_to_all | solution.py:439
  86.2 0.6 select_reduce_fusion
  86.8 19.3 %all-gather.6.cloned.1.call-done = bf16[512,2048]{1,0:T(8,128)(2,1)} async-done(((bf16[128,2048]{1,0:T(8,128)(2,1)}), bf16[512,2048]{1,0:T(8,128)(2,1)}) %all-gather.6.cloned.1.call-update) | async-done | bytes 2097168 | tf_op jit(solution)/shard_map/all_gather | solution.py:442
  106.2 2.2 multiply_reduce_fusion
  108.4 1.0 copy-done.1
  109.4 0.9 multiply_convert_fusion.2.x_ref
  110.3 55.5 %gather_rows.1 = (bf16[16,128,2048]{2,1,0:T(8,128)(2,1)}, f32[16,16,128]{2,1,0:T(8,128)}) custom-call(bf16[128,2048]{1,0:T(8,128)(2,1)} %multiply_convert_fusion.2.x_ref, f32[16,128]{1,0:T(8,128)} %bitcast.102), custom_call_target="tpu_custom_call" | custom-call | tf_op jit(solution)/shard_map/gather_rows/pallas_call | solution.py:310
  165.8 0.9 constant_dynamic-slice_fusion
  166.7 11.7 %fusion.3 = f32[2048,768]{1,0:T(8,128)} fusion(bf16[2048,2048]{1,0:T(8,128)(2,1)} %bitcast.104, bf16[1,2048,768]{2,1,0:T(8,128)(2,1)} %param.17), kind=kOutput, calls=%fused_computation.5 | convolution fusion | flops 6442450944 | bytes 17825792 | tf_op jit(solution)/shard_map/dot_general | solution.py:364
  178.4 20.6 %multiply_convert_fusion = bf16[2048,2048]{1,0:T(8,128)(2,1)} fusion(f32[2048]{0:T(1024)S(1)} %bitcast.103, f32[2048,768]{1,0:T(8,128)} %fusion.3, bf16[2048,2048]{1,0:T(8,128)(2,1)} %bitcast.105, bf16[1,768,2048]{2,1,0:T(8,128)(2,1)S(1)} %copy-done, bf16[1,2048,768]{2,1,0:T(8,128)(2,1)} %param.18), kind=kOutput, calls=%fused_computation.1 | convolution fusion | flops 12902727680 | bytes 29368320 | tf_op jit(solution)/shard_map/dot_general | solution.py:367
  199.0 58.5 %scatter_sums.1 = f32[128,2048]{1,0:T(8,128)} custom-call(bf16[16,128,2048]{2,1,0:T(8,128)(2,1)} %bitcast.87), custom_call_target="tpu_custom_call" | custom-call | tf_op jit(solution)/shard_map/scatter_sums/pallas_call | solution.py:335
  257.5 2.5 add_convert_fusion
  (24 shorter events, 0.1 us)
Async XLA Ops:
  6.5 171.9 %copy-start = (bf16[1,768,2048]{2,1,0:T(8,128)(2,1)S(1)}, bf16[1,768,2048]{2,1,0:T(8,128)(2,1)}, u32[]{:S(2)}) copy-start(bf16[1,768,2048]{2,1,0:T(8,128)(2,1)} %param.19) | copy-start | bytes 9437188
  6.5 50.8 %all-gather.4.cloned.1.call-start = ((), (), s32[]{:S(2)}) async-start(), calls=%async_computation.1 | async-start | bytes 2621440 | tf_op jit(solution)/shard_map/all_gather | solution.py:384
  7.3 98.9 %all-gather.6.cloned.1.call-start = ((), (), s32[]{:S(2)}) async-start(), calls=%async_computation.2 | async-start | bytes 2621440 | tf_op jit(solution)/shard_map/all_gather | solution.py:442
  57.3 16.7 %copy-start.4 = (f32[1,128,128]{2,1,0:T(8,128)S(1)}, f32[1,128,128]{2,1,0:T(8,128)}, u32[]{:S(2)}) copy-start(f32[1,128,128]{2,1,0:T(8,128)} %param.13) | copy-start | bytes 196612
  60.4 6.3 %copy-start.3 = (bf16[512,384]{0,1:T(8,128)(2,1)}, bf16[512,384]{0,1:T(8,128)(2,1)S(1)}, u32[]{:S(2)}) copy-start(bf16[512,384]{0,1:T(8,128)(2,1)S(1)} %convolution_convert_fusion) | copy-start | bytes 1179652
  71.1 7.3 %collective-permute-start = (bf16[2,1,512,128]{3,2,1,0:T(8,128)(2,1)}, bf16[2,1,512,128]{3,2,1,0:T(8,128)(2,1)}, u32[]{:S(2)}, u32[]{:S(2)}) collective-permute-start(bf16[2,1,512,128]{3,2,1,0:T(8,128)(2,1)} %pad_maximum_fusion), channel_id=1, source_target_pairs={{0,4},{4,8},{8,12},{1,5},{5,9},{9,13},{2,6},{6,10},{10,14},{3,7},{... | collective-permute-start | bytes 786440 | tf_op jit(solution)/shard_map/ppermute | solution.py:29
  74.0 5.4 %copy-start.2 = (bf16[512,1,1,128]{3,0,2,1:T(8,128)(2,1)S(1)}, bf16[512,1,1,128]{3,0,2,1:T(8,128)(2,1)}, u32[]{:S(2)}) copy-start(bf16[512,1,1,128]{3,0,2,1:T(8,128)(2,1)} %copy.34) | copy-start | bytes 393220
  79.4 2.1 copy-start.7
  81.5 4.7 %copy-start.5 = (f32[128,8]{0,1:T(8,128)S(1)}, f32[128,8]{0,1:T(8,128)}, u32[]{:S(2)}) copy-start(f32[128,8]{0,1:T(8,128)} %param.21) | copy-start | bytes 12292
  81.5 4.7 %copy-start.6 = (s32[128,8]{0,1:T(8,128)S(1)}, s32[128,8]{0,1:T(8,128)}, u32[]{:S(2)}) copy-start(s32[128,8]{0,1:T(8,128)} %param.20) | copy-start | bytes 12292
  82.9 23.3 %all-to-all-start = ((bf16[4,128,128]{1,2,0:T(8,128)(2,1)}), bf16[4,128,128]{1,2,0:T(8,128)(2,1)S(1)}, u32[]{:S(2)}, u32[]{:S(2)}) async-start(bf16[4,128,128]{1,2,0:T(8,128)(2,1)} %copy.33), calls=%async_computation | async-start | bytes 262144 | tf_op jit(solution)/shard_map/all_to_all | solution.py:439
  108.4 1.0 copy-start.1
Sparse Core Ops, SparseCore 0:
  8.9 48.3 all-gather.3
  58.9 47.2 all-gather.5

commit v3 on v2

--- a/solution.py
+++ b/solution.py
@@ -36,6 +36,7 @@
 MESH = pl.DeviceIdType.MESH
 VMEM_BYTES = 60 * 1024 * 1024
 ADD_ROWS = 16
+DOT_COLUMNS = 512
 
 
 def place(count):
@@ -177,7 +178,7 @@
 
 
 def scatter_kernel(
-    count, part_ref, out_ref, from_beside, from_across, below, above, to_across, to_line,
+    count, hid_ref, down_ref, out_ref, part_ref, from_beside, from_across, below, above, to_across, to_line,
     beside_send, beside_recv, across_send, across_recv, line_send, below_recv, above_recv,
 ):
     z, c, beside, across, diagonal = place(count)
@@ -190,11 +191,28 @@
             def _():
                 act(z + d, 1)
 
+        for d in range(count - 1, 0, -1):
+
             @pl.when(z >= d)
             def _():
                 act(z - d, -1)
 
         act(z, 0)
+
+    def nth(index):
+        ups = count - 1 - z
+        downs = jnp.where(index < count - 1, index - ups, z)
+        return jnp.where(index < ups, count - 1 - index, downs)
+
+    def compute(slot):
+        def tile(index, _):
+            columns = pl.ds(pl.multiple_of(index * DOT_COLUMNS, DOT_COLUMNS), DOT_COLUMNS)
+            part_ref[slot, :, columns] = jnp.dot(
+                hid_ref[slot], down_ref[:, columns], preferred_element_type=jnp.float32
+            ).astype(part_ref.dtype)
+            return 0
+
+        lax.fori_loop(0, down_ref.shape[1] // DOT_COLUMNS, tile, 0)
 
     def beside_copy(kind, zz):
         cc = diagonal if kind == 0 else beside
@@ -248,15 +266,20 @@
 
         lax.fori_loop(0, target.shape[0] // ADD_ROWS, chunk, 0)
 
-    by_distance(lambda zz, side: beside_copy(0, zz).start())
-    by_distance(lambda zz, side: beside_copy(1, zz).start())
-
-    def pass_across(zz, side):
+    def project(index, _):
+        zz = nth(index)
+        compute(diagonal * count + zz)
+        beside_copy(0, zz).start()
+        compute(across * count + zz)
         beside_copy(0, zz).wait_recv()
         add(to_across.at[zz], [part_ref.at[across * count + zz], from_beside.at[0, zz]])
         across_copy(zz).start()
-
-    by_distance(pass_across)
+        compute(beside * count + zz)
+        beside_copy(1, zz).start()
+        compute(c * count + zz)
+        return 0
+
+    lax.fori_loop(0, count, project, 0)
 
     def pass_line(zz, side):
         beside_copy(1, zz).wait_recv()
@@ -327,25 +350,37 @@
     )(normed, table)
 
 
-def scatter_sums(parts):
+def scatter_sums(hid, down):
     count = lax.axis_size("heads")
-    _, rows, width = parts.shape
-    block = (rows, width)
+    devices, rows, _ = hid.shape
+    block = (rows, down.shape[1])
     dma = pltpu.SemaphoreType.DMA
     return pl.pallas_call(
         functools.partial(scatter_kernel, count),
         out_shape=jax.ShapeDtypeStruct(block, jnp.float32),
-        in_specs=[pl.BlockSpec(memory_space=pltpu.VMEM)],
+        in_specs=[pl.BlockSpec(memory_space=pltpu.VMEM)] * 2,
         out_specs=pl.BlockSpec(memory_space=pltpu.VMEM),
-        scratch_shapes=[pltpu.VMEM((2, count) + block, parts.dtype)]
-        + [pltpu.VMEM((count,) + block, parts.dtype)] * 5
+        scratch_shapes=[
+            pltpu.VMEM((devices,) + block, hid.dtype),
+            pltpu.VMEM((2, count) + block, hid.dtype),
+        ]
+        + [pltpu.VMEM((count,) + block, hid.dtype)] * 5
         + [dma((2, count))] * 2
         + [dma((count,))] * 5,
         compiler_params=pltpu.CompilerParams(
             collective_id=1, has_side_effects=True, vmem_limit_bytes=VMEM_BYTES
         ),
         name="scatter_sums",
-    )(parts)
+    )(hid, down)
+
+
+def whole_rows(w_out):
+    ctx_count, rows = lax.axis_size("ctx"), w_out.shape[0]
+    share = rows // ctx_count
+    if rows % ctx_count or share % 16:
+        return lax.all_gather(w_out, "heads", axis=0, tiled=True)
+    mine = lax.dynamic_slice_in_dim(w_out, lax.axis_index("ctx") * share, share, 0)
+    return lax.all_gather(mine, ("heads", "ctx"), axis=0, tiled=True)
 
 
 def dense_experts(
@@ -359,17 +394,16 @@
     rows, tables = gather_rows(normed, table.T)
     device_count, row_count, width = rows.shape
     rows = rows.reshape(device_count * row_count, width)
-    total = None
+    hids = []
     for e in range(exp_local):
         gate_act = jnp.dot(rows, w_gate[e], preferred_element_type=jnp.float32)
         up_act = jnp.dot(rows, w_up[e], preferred_element_type=jnp.float32)
-        hid = (jax.nn.silu(gate_act) * up_act).astype(jnp.bfloat16)
-        out_rows = jnp.dot(hid, w_down[e], preferred_element_type=jnp.float32)
         weight = lax.dynamic_slice_in_dim(tables, first + e, 1, 1).reshape(-1, 1)
-        part = weight * out_rows
-        total = part if total is None else total + part
-    parts = total.astype(jnp.bfloat16).reshape(device_count, row_count, width)
-    routed = scatter_sums(parts)
+        hids.append((weight * (jax.nn.silu(gate_act) * up_act)).astype(jnp.bfloat16))
+    hid = jnp.concatenate(hids, axis=1) if exp_local > 1 else hids[0]
+    routed = scatter_sums(
+        hid.reshape(device_count, row_count, hid.shape[1]), w_down.reshape(hid.shape[1], width)
+    )
     return (hidden_float + routed).astype(jnp.bfloat16)
 
 
@@ -439,7 +473,7 @@
     regrouped = lax.all_to_all(heads_out, "heads", split_axis=0, concat_axis=1, tiled=True)
     attn = jnp.dot(
         regrouped,
-        lax.all_gather(w_out, "heads", axis=0, tiled=True),
+        whole_rows(w_out),
         preferred_element_type=jnp.float32,
     )
     hidden_state = (tokens.astype(jnp.float32) + attn).astype(jnp.bfloat16)

time: 267 us -> 267 us (level)
  Pallas kernels: 114 us -> 133 us
  matrix products: 44.1 us -> 31.4 us
  waiting for transfers between devices: 67.4 us -> 61.6 us
    pallas_call x1, Pallas kernels: 58.5 us -> 76 us  [scatter_sums(): pl.pallas_call(functools.partial(scatter_kernel, count), out_shape=jax.Sh...]
    all_gather x1, waiting for transfers between devices: 19.3 us -> 5.82 us  [whole_rows(): return lax.all_gather(mine, ('heads', 'ctx'), axis=0, tiled=True)]
    dot_general x2, matrix products: 22.8 us -> 11 us  [the longest x1 8.76 us: dense_experts(): up_act = jnp.dot(rows, w_up[e], preferred_element_type=jnp.float32)]
    all_to_all x1, waiting for transfers between devices: 0.01 us -> 9.49 us  [on_device(): lax.all_to_all(heads_out, 'heads', split_axis=0, concat_axis=1, tiled=True)]
    unnamed x19 -> x25, local copies, waits for them, and re-layouts: 6.33 us -> 5.39 us
  transfers between devices with their start and end apart: 4 -> 4, of which waited for: 2 -> 3; matrix products, arithmetic and copies ran while one was open for 8% -> 8% of each run, Pallas kernels for 0% -> 0%
where the time goes in v3:
time: 267 us; the launch traced here: 266 us
  Pallas kernels  133 us (50%)
  waiting for transfers between devices  61.6 us (23%)
  matrix products  31.4 us (12%)
  between operations  13.6 us (5%)
  local copies, waits for them, and re-layouts  9.45 us (4%)
  other arithmetic  6.33 us (2%)
  starting transfers between devices  5.93 us (2%)
  blocking collectives  5.49 us (2%)
    pallas_call x1, Pallas kernels, scatter_sums(): pl.pallas_call(functools.partial(scatter_kernel, count), out_shape=jax.Sh...  76 us
    pallas_call x1, Pallas kernels, gather_rows(): pl.pallas_call(functools.partial(gather_kernel, count), out_shape=[jax.Sh...  56.6 us
    all_gather x1, waiting for transfers between devices, on_device(): lax.all_gather(tokens, 'heads', axis=0, tiled=True)  45.6 us
    dot_general x1, matrix products, dense_experts(): gate_act = jnp.dot(rows, w_gate[e], preferred_element_type=jnp.float32)  9.84 us
    all_to_all x1, waiting for transfers between devices, on_device(): lax.all_to_all(heads_out, 'heads', split_axis=0, concat_axis=1, tiled=True)  9.49 us
    dot_general x1, matrix products, dense_experts(): up_act = jnp.dot(rows, w_up[e], preferred_element_type=jnp.float32)  8.76 us
    all_gather x1, waiting for transfers between devices, whole_rows(): return lax.all_gather(mine, ('heads', 'ctx'), axis=0, tiled=True)  5.82 us
    all_gather x1, blocking collectives, entering(): gathered = lax.all_gather(x.astype(jnp.bfloat16), axis)  5.49 us
  transfers between devices with their start and end apart: 4, of which 3 were waited for; matrix products, arithmetic and copies ran while one was open for 8% of the time, Pallas kernels for 0%

profile of v3, /device:TPU:0, one launch (start us, length us, event | category | flops | bytes accessed | tf_op | source)
XLA Modules:
  0.0 266.4 jit_solution(944194982610696876)
XLA Ops:
  6.5 0.7 all-gather.4.cloned.1.call-update
  7.3 1.7 constant_dynamic-slice_fusion.1
  9.1 2.6 copy.27
  11.7 45.6 %all-gather.4.cloned.1.call-done = bf16[512,2048]{1,0:T(8,128)(2,1)} async-done(((bf16[128,2048]{1,0:T(8,128)(2,1)}), bf16[512,2048]{1,0:T(8,128)(2,1)}) %all-gather.4.cloned.1.call-update) | async-done | bytes 2097168 | tf_op jit(solution)/shard_map/all_gather | solution.py:418
  57.3 3.0 %convolution_convert_fusion = bf16[512,384]{0,1:T(8,128)(2,1)S(1)} fusion(bf16[512,2048]{1,0:T(8,128)(2,1)} %all-gather.4.cloned.1.call-done, bf16[2048,384]{0,1:T(8,128)(2,1)} %bitcast.86), kind=kOutput, calls=%fused_computation.18 | convolution fusion | flops 805502976 | bytes 4063232 | tf_op jit(solution)/shard_map/dot_general | solution.py:417
  60.4 0.7 fusion.34
  61.3 1.0 copy.34
  62.3 0.8 pad_maximum_fusion
  63.1 2.3 collective-permute-start
  65.4 1.2 convolution_convert_fusion.1
  66.5 5.5 %all-gather = bf16[512,128]{1,0:T(8,128)(2,1)S(1)} all-gather(bf16[128,128]{1,0:T(8,128)(2,1)S(1)} %convolution_convert_fusion.1), channel_id=2, replica_groups=mesh['groups'=2,'ctx'=4,'heads'=4] {'ctx'}, dimensions={0}, use_global_device_ids=true | all-gather | bytes 163840 | tf_op jit(solution)/shard_map/all_gather | solution.py:17
  72.0 2.0 fusion.23
  74.0 2.3 multiply_reduce_fusion.1
  76.3 1.1 bitcast_select_fusion
  77.4 1.5 fusion.35
  78.9 0.5 fusion.8
  79.4 0.4 copy-done.10
  79.9 0.6 fusion.12
  80.4 0.8 copy.33
  81.2 3.6 %all-to-all-start = ((bf16[4,128,128]{1,2,0:T(8,128)(2,1)}), bf16[4,128,128]{1,2,0:T(8,128)(2,1)S(1)}, u32[]{:S(2)}, u32[]{:S(2)}) async-start(bf16[4,128,128]{1,2,0:T(8,128)(2,1)} %copy.33), calls=%async_computation | async-start | bytes 262144 | tf_op jit(solution)/shard_map/all_to_all | solution.py:473
  84.8 0.6 select_reduce_fusion
  85.5 9.5 %all-to-all-done = bf16[4,128,128]{1,2,0:T(8,128)(2,1)S(1)} async-done(((bf16[4,128,128]{1,2,0:T(8,128)(2,1)}), bf16[4,128,128]{1,2,0:T(8,128)(2,1)S(1)}, u32[]{:S(2)}, u32[]{:S(2)}) %all-to-all-start) | async-done | bytes 131104 | tf_op jit(solution)/shard_map/all_to_all | solution.py:473
  94.9 5.8 %all-gather.6.cloned.1.call-done = bf16[512,2048]{1,0:T(8,128)(2,1)} async-done(((bf16[32,2048]{1,0:T(8,128)(2,1)}), bf16[512,2048]{1,0:T(8,128)(2,1)}) %all-gather.6.cloned.1.call-update) | async-done | bytes 2097168 | tf_op jit(solution)/shard_map/all_gather | solution.py:383
  100.8 2.2 multiply_reduce_fusion
  103.0 1.0 copy-done.1
  104.1 0.9 multiply_convert_fusion.1.x_ref
  105.0 56.6 %gather_rows.1 = (bf16[16,128,2048]{2,1,0:T(8,128)(2,1)}, f32[16,16,128]{2,1,0:T(8,128)}) custom-call(bf16[128,2048]{1,0:T(8,128)(2,1)} %multiply_convert_fusion.1.x_ref, f32[16,128]{1,0:T(8,128)} %bitcast.100), custom_call_target="tpu_custom_call" | custom-call | tf_op jit(solution)/shard_map/gather_rows/pallas_call | solution.py:333
  161.6 0.9 constant_dynamic-slice_fusion
  162.5 9.8 %fusion.1 = f32[2048,768]{1,0:T(8,128)S(1)} fusion(bf16[2048,2048]{1,0:T(8,128)(2,1)} %bitcast.102, bf16[1,2048,768]{2,1,0:T(8,128)(2,1)S(1)} %copy-done), kind=kOutput, calls=%fused_computation.3 | convolution fusion | flops 6442450944 | bytes 17825792 | tf_op jit(solution)/shard_map/dot_general | solution.py:399
  172.4 8.8 %multiply_convert_fusion = bf16[2048,768]{1,0:T(8,128)(2,1)} fusion(f32[2048,768]{1,0:T(8,128)S(1)} %fusion.1, bf16[2048,2048]{1,0:T(8,128)(2,1)S(1)} %bitcast.103, bf16[1,2048,768]{2,1,0:T(8,128)(2,1)S(1)} %copy-done.9, f32[2048]{0:T(1024)S(1)} %bitcast.101), kind=kOutput, calls=%fused_computation.1 | convolution fusion | flops 6453460992 | bytes 20979712 | tf_op jit(solution)/shard_map/dot_general | solution.py:400
  181.1 76.0 %scatter_sums.1 = f32[128,2048]{1,0:T(8,128)} custom-call(bf16[16,128,768]{2,1,0:T(8,128)(2,1)} %bitcast.85, bf16[768,2048]{1,0:T(8,128)(2,1)} %bitcast.84), custom_call_target="tpu_custom_call" | custom-call | tf_op jit(solution)/shard_map/scatter_sums/pallas_call | solution.py:358
  257.1 2.5 add_convert_fusion
  (31 shorter events, 0.4 us)
Async XLA Ops:
  6.5 155.9 %copy-start = (bf16[1,2048,768]{2,1,0:T(8,128)(2,1)S(1)}, bf16[1,2048,768]{2,1,0:T(8,128)(2,1)}, u32[]{:S(2)}) copy-start(bf16[1,2048,768]{2,1,0:T(8,128)(2,1)} %param.17) | copy-start | bytes 9437188
  6.5 50.8 %all-gather.4.cloned.1.call-start = ((), (), s32[]{:S(2)}) async-start(), calls=%async_computation.1 | async-start | bytes 2621440 | tf_op jit(solution)/shard_map/all_gather | solution.py:418
  7.3 93.5 %all-gather.6.cloned.1.call-start = ((), (), s32[]{:S(2)}) async-start(), calls=%async_computation.2 | async-start | bytes 2228224 | tf_op jit(solution)/shard_map/all_gather | solution.py:383
  60.4 0.8 copy-start.4
  60.4 11.7 %copy-start.5 = (f32[1,128,128]{2,1,0:T(8,128)S(1)}, f32[1,128,128]{2,1,0:T(8,128)}, u32[]{:S(2)}) copy-start(f32[1,128,128]{2,1,0:T(8,128)} %param.13) | copy-start | bytes 196612
  62.3 3.0 %copy-start.2 = (bf16[512,1,1,128]{3,0,2,1:T(8,128)(2,1)}, bf16[512,1,1,128]{3,0,2,1:T(8,128)(2,1)S(1)}, u32[]{:S(2)}) copy-start(bf16[512,1,1,128]{3,0,2,1:T(8,128)(2,1)S(1)} %copy.34) | copy-start | bytes 393220
  63.1 13.3 %collective-permute-start = (bf16[2,1,512,128]{3,2,1,0:T(8,128)(2,1)}, bf16[2,1,512,128]{3,2,1,0:T(8,128)(2,1)}, u32[]{:S(2)}, u32[]{:S(2)}) collective-permute-start(bf16[2,1,512,128]{3,2,1,0:T(8,128)(2,1)} %pad_maximum_fusion), channel_id=1, source_target_pairs={{0,4},{4,8},{8,12},{1,5},{5,9},{9,13},{2,6},{6,10},{10,14},{3,7},{... | collective-permute-start | bytes 786440 | tf_op jit(solution)/shard_map/ppermute | solution.py:29
  72.0 5.4 %copy-start.3 = (bf16[512,1,1,128]{3,0,2,1:T(8,128)(2,1)S(1)}, bf16[512,1,1,128]{3,0,2,1:T(8,128)(2,1)}, u32[]{:S(2)}) copy-start(bf16[512,1,1,128]{3,0,2,1:T(8,128)(2,1)} %copy-done.2) | copy-start | bytes 393220
  78.9 1.0 copy-start.10
  79.9 5.0 %copy-start.6 = (f32[128,8]{0,1:T(8,128)S(1)}, f32[128,8]{0,1:T(8,128)}, u32[]{:S(2)}) copy-start(f32[128,8]{0,1:T(8,128)} %param.21) | copy-start | bytes 12292
  79.9 5.0 %copy-start.7 = (s32[128,8]{0,1:T(8,128)S(1)}, s32[128,8]{0,1:T(8,128)}, u32[]{:S(2)}) copy-start(s32[128,8]{0,1:T(8,128)} %param.20) | copy-start | bytes 12292
  81.2 13.7 %all-to-all-start = ((bf16[4,128,128]{1,2,0:T(8,128)(2,1)}), bf16[4,128,128]{1,2,0:T(8,128)(2,1)S(1)}, u32[]{:S(2)}, u32[]{:S(2)}) async-start(bf16[4,128,128]{1,2,0:T(8,128)(2,1)} %copy.33), calls=%async_computation | async-start | bytes 262144 | tf_op jit(solution)/shard_map/all_to_all | solution.py:473
  103.0 1.1 copy-start.1
  162.5 9.9 %copy-start.8 = (bf16[16,128,2048]{2,1,0:T(8,128)(2,1)S(1)}, bf16[16,128,2048]{2,1,0:T(8,128)(2,1)}, u32[]{:S(2)}) copy-start(bf16[16,128,2048]{2,1,0:T(8,128)(2,1)} %get-tuple-element.62) | copy-start | bytes 25165828
  162.5 9.9 %copy-start.9 = (bf16[1,2048,768]{2,1,0:T(8,128)(2,1)S(1)}, bf16[1,2048,768]{2,1,0:T(8,128)(2,1)}, u32[]{:S(2)}) copy-start(bf16[1,2048,768]{2,1,0:T(8,128)(2,1)} %param.18) | copy-start | bytes 9437188
Sparse Core Ops, SparseCore 0:
  8.9 48.3 all-gather.3
  59.5 41.2 all-gather.5

commit v4 on v3

--- a/solution.py
+++ b/solution.py
@@ -37,6 +37,7 @@
 VMEM_BYTES = 60 * 1024 * 1024
 ADD_ROWS = 16
 DOT_COLUMNS = 512
+LAG = 2
 
 
 def place(count):
@@ -178,38 +179,31 @@
 
 
 def scatter_kernel(
-    count, hid_ref, down_ref, out_ref, part_ref, from_beside, from_across, below, above, to_across, to_line,
+    count, hid_ref, down_ref, weight_ref, out_ref, part_ref, from_beside, from_across, below, above, to_across, to_line,
     beside_send, beside_recv, across_send, across_recv, line_send, below_recv, above_recv,
 ):
     z, c, beside, across, diagonal = place(count)
     greet(z, count, beside, across)
 
-    def by_distance(act):
-        for d in range(count - 1, 0, -1):
-
-            @pl.when(z + d < count)
-            def _():
-                act(z + d, 1)
-
-        for d in range(count - 1, 0, -1):
-
-            @pl.when(z >= d)
-            def _():
-                act(z - d, -1)
-
-        act(z, 0)
-
     def nth(index):
-        ups = count - 1 - z
-        downs = jnp.where(index < count - 1, index - ups, z)
-        return jnp.where(index < ups, count - 1 - index, downs)
+        more = jnp.maximum(z, count - 1 - z)
+        fewer = count - 1 - more
+        alone = more - fewer
+        paired = jnp.maximum(index - alone, 0)
+        up = jnp.where(z + more < count, more - index, index - more)
+        both = (fewer - paired // 2) * (1 - 2 * (paired % 2))
+        offset = jnp.where(index < alone, up, both)
+        return z + jnp.where(index < count - 1, offset, 0)
 
     def compute(slot):
+        weight = weight_ref[slot][:, :1]
+
         def tile(index, _):
             columns = pl.ds(pl.multiple_of(index * DOT_COLUMNS, DOT_COLUMNS), DOT_COLUMNS)
-            part_ref[slot, :, columns] = jnp.dot(
+            product = jnp.dot(
                 hid_ref[slot], down_ref[:, columns], preferred_element_type=jnp.float32
-            ).astype(part_ref.dtype)
+            )
+            part_ref[slot, :, columns] = (weight * product).astype(part_ref.dtype)
             return 0
 
         lax.fori_loop(0, down_ref.shape[1] // DOT_COLUMNS, tile, 0)
@@ -266,8 +260,7 @@
 
         lax.fori_loop(0, target.shape[0] // ADD_ROWS, chunk, 0)
 
-    def project(index, _):
-        zz = nth(index)
+    def project(zz):
         compute(diagonal * count + zz)
         beside_copy(0, zz).start()
         compute(across * count + zz)
@@ -277,15 +270,34 @@
         compute(beside * count + zz)
         beside_copy(1, zz).start()
         compute(c * count + zz)
-        return 0
-
-    lax.fori_loop(0, count, project, 0)
-
-    def pass_line(zz, side):
+
+    def onward(zz, copy, arriving, first, sources):
+        @pl.when(first)
+        def _():
+            add(to_line.at[zz], sources)
+
+        @pl.when(jnp.logical_not(first))
+        def _():
+            copy(zz).wait_recv()
+            add(to_line.at[zz], sources + [arriving.at[zz]])
+
+        copy(zz).start()
+
+    def pass_line(zz):
         beside_copy(1, zz).wait_recv()
         across_copy(zz).wait_recv()
         sources = [part_ref.at[c * count + zz], from_beside.at[1, zz], from_across.at[zz]]
-        if side == 0:
+
+        @pl.when(zz > z)
+        def _():
+            onward(zz, up_copy, below, z == 0, sources)
+
+        @pl.when(zz < z)
+        def _():
+            onward(zz, down_copy, above, z == count - 1, sources)
+
+        @pl.when(zz == z)
+        def _():
             add(out_ref, sources)
 
             @pl.when(z > 0)
@@ -298,34 +310,31 @@
                 down_copy(zz).wait_recv()
                 add(out_ref, [out_ref, above.at[zz]])
 
-            return
-        first = z == 0 if side > 0 else z == count - 1
-        copy = up_copy if side > 0 else down_copy
-        arriving = below if side > 0 else above
-
-        @pl.when(first)
-        def _():
-            add(to_line.at[zz], sources)
-
-        @pl.when(jnp.logical_not(first))
-        def _():
-            copy(zz).wait_recv()
-            add(to_line.at[zz], sources + [arriving.at[zz]])
-
-        copy(zz).start()
-
-    by_distance(pass_line)
-
-    def sent(zz, side):
+    def step(index, _):
+        @pl.when(index < count)
+        def _():
+            project(nth(index))
+
+        @pl.when(index >= LAG)
+        def _():
+            pass_line(nth(index - LAG))
+
+        return 0
+
+    lax.fori_loop(0, count + LAG, step, 0)
+
+    for zz in range(count):
         beside_copy(0, zz).wait_send()
         beside_copy(1, zz).wait_send()
         across_copy(zz).wait_send()
-        if side > 0:
+
+        @pl.when(zz > z)
+        def _():
             up_copy(zz).wait_send()
-        if side < 0:
+
+        @pl.when(zz < z)
+        def _():
             down_copy(zz).wait_send()
-
-    by_distance(sent)
 
 
 def gather_rows(normed, table):
@@ -350,7 +359,7 @@
     )(normed, table)
 
 
-def scatter_sums(hid, down):
+def scatter_sums(hid, down, weights):
     count = lax.axis_size("heads")
     devices, rows, _ = hid.shape
     block = (rows, down.shape[1])
@@ -358,7 +367,7 @@
     return pl.pallas_call(
         functools.partial(scatter_kernel, count),
         out_shape=jax.ShapeDtypeStruct(block, jnp.float32),
-        in_specs=[pl.BlockSpec(memory_space=pltpu.VMEM)] * 2,
+        in_specs=[pl.BlockSpec(memory_space=pltpu.VMEM)] * 3,
         out_specs=pl.BlockSpec(memory_space=pltpu.VMEM),
         scratch_shapes=[
             pltpu.VMEM((devices,) + block, hid.dtype),
@@ -371,7 +380,7 @@
             collective_id=1, has_side_effects=True, vmem_limit_bytes=VMEM_BYTES
         ),
         name="scatter_sums",
-    )(hid, down)
+    )(hid, down, weights)
 
 
 def whole_rows(w_out):
@@ -394,16 +403,15 @@
     rows, tables = gather_rows(normed, table.T)
     device_count, row_count, width = rows.shape
     rows = rows.reshape(device_count * row_count, width)
-    hids = []
+    routed = 0.0
     for e in range(exp_local):
         gate_act = jnp.dot(rows, w_gate[e], preferred_element_type=jnp.float32)
         up_act = jnp.dot(rows, w_up[e], preferred_element_type=jnp.float32)
-        weight = lax.dynamic_slice_in_dim(tables, first + e, 1, 1).reshape(-1, 1)
-        hids.append((weight * (jax.nn.silu(gate_act) * up_act)).astype(jnp.bfloat16))
-    hid = jnp.concatenate(hids, axis=1) if exp_local > 1 else hids[0]
-    routed = scatter_sums(
-        hid.reshape(device_count, row_count, hid.shape[1]), w_down.reshape(hid.shape[1], width)
-    )
+        hid = (jax.nn.silu(gate_act) * up_act).astype(jnp.bfloat16)
+        weight = lax.dynamic_index_in_dim(tables, first + e, 1, False)
+        weight = jnp.broadcast_to(weight[:, :, None], (device_count, row_count, HDIM))
+        hid = hid.reshape(device_count, row_count, hid.shape[1])
+        routed = routed + scatter_sums(hid, w_down[e], weight)
     return (hidden_float + routed).astype(jnp.bfloat16)
 
 

time: 267 us -> 251 us (0.940)
  Pallas kernels: 133 us -> 115 us
    pallas_call x1, Pallas kernels: 76 us -> 58.8 us  [scatter_sums(): pl.pallas_call(functools.partial(scatter_kernel, count), out_shape=jax.Sh...]
where the time goes in v4:
time: 251 us; the launch traced here: 250 us
  Pallas kernels  115 us (46%)
  waiting for transfers between devices  61.6 us (25%)
  matrix products  31.1 us (12%)
  between operations  13.6 us (5%)
  local copies, waits for them, and re-layouts  10.8 us (4%)
  other arithmetic  6.29 us (3%)
  starting transfers between devices  5.94 us (2%)
  blocking collectives  5.49 us (2%)
    pallas_call x1, Pallas kernels, scatter_sums(): pl.pallas_call(functools.partial(scatter_kernel, count), out_shape=jax.Sh...  58.8 us
    pallas_call x1, Pallas kernels, gather_rows(): pl.pallas_call(functools.partial(gather_kernel, count), out_shape=[jax.Sh...  56.6 us
    all_gather x1, waiting for transfers between devices, on_device(): lax.all_gather(tokens, 'heads', axis=0, tiled=True)  45.6 us
    dot_general x1, matrix products, dense_experts(): gate_act = jnp.dot(rows, w_gate[e], preferred_element_type=jnp.float32)  9.84 us
    all_to_all x1, waiting for transfers between devices, on_device(): lax.all_to_all(heads_out, 'heads', split_axis=0, concat_axis=1, tiled=True)  9.47 us
    dot_general x1, matrix products, dense_experts(): up_act = jnp.dot(rows, w_up[e], preferred_element_type=jnp.float32)  8.53 us
    all_gather x1, waiting for transfers between devices, whole_rows(): return lax.all_gather(mine, ('heads', 'ctx'), axis=0, tiled=True)  5.84 us
    all_gather x1, blocking collectives, entering(): gathered = lax.all_gather(x.astype(jnp.bfloat16), axis)  5.49 us
  transfers between devices with their start and end apart: 4, of which 3 were waited for; matrix products, arithmetic and copies ran while one was open for 8% of the time, Pallas kernels for 0%

profile of v4, /device:TPU:0, one launch (start us, length us, event | category | flops | bytes accessed | tf_op | source)
XLA Modules:
  0.0 250.4 jit_solution(964843497926588182)
XLA Ops:
  6.5 0.7 all-gather.4.cloned.1.call-update
  7.3 1.7 constant_dynamic-slice_fusion.1
  9.1 2.6 %copy.27 = bf16[2048,3,128]{0,2,1:T(8,128)(2,1)} copy(bf16[2048,3,128]{2,0,1:T(8,128)(2,1)} %param.15) | data formatting | bytes 3145728 | tf_op args[3]
  11.7 45.6 %all-gather.4.cloned.1.call-done = bf16[512,2048]{1,0:T(8,128)(2,1)} async-done(((bf16[128,2048]{1,0:T(8,128)(2,1)}), bf16[512,2048]{1,0:T(8,128)(2,1)}) %all-gather.4.cloned.1.call-update) | async-done | bytes 2097168 | tf_op jit(solution)/shard_map/all_gather | solution.py:426
  57.3 3.0 %convolution_convert_fusion = bf16[512,384]{0,1:T(8,128)(2,1)S(1)} fusion(bf16[512,2048]{1,0:T(8,128)(2,1)} %all-gather.4.cloned.1.call-done, bf16[2048,384]{0,1:T(8,128)(2,1)} %bitcast.86), kind=kOutput, calls=%fused_computation.18 | convolution fusion | flops 805502976 | bytes 4063232 | tf_op jit(solution)/shard_map/dot_general | solution.py:425
  60.4 0.7 fusion.34
  61.3 1.1 copy.35
  62.4 0.7 pad_maximum_fusion
  63.1 2.3 collective-permute-start
  65.4 1.2 convolution_convert_fusion.1
  66.5 5.5 %all-gather = bf16[512,128]{1,0:T(8,128)(2,1)S(1)} all-gather(bf16[128,128]{1,0:T(8,128)(2,1)S(1)} %convolution_convert_fusion.1), channel_id=2, replica_groups=mesh['groups'=2,'ctx'=4,'heads'=4] {'ctx'}, dimensions={0}, use_global_device_ids=true | all-gather | bytes 163840 | tf_op jit(solution)/shard_map/all_gather | solution.py:17
  72.0 2.0 fusion.23
  74.0 2.3 multiply_reduce_fusion.1
  76.3 1.1 bitcast_select_fusion
  77.4 1.5 fusion.35
  78.9 0.5 fusion.8
  79.9 0.6 fusion.12
  80.4 0.8 copy.33
  81.2 3.6 %all-to-all-start = ((bf16[4,128,128]{1,2,0:T(8,128)(2,1)}), bf16[4,128,128]{1,2,0:T(8,128)(2,1)S(1)}, u32[]{:S(2)}, u32[]{:S(2)}) async-start(bf16[4,128,128]{1,2,0:T(8,128)(2,1)} %copy.33), calls=%async_computation | async-start | bytes 262144 | tf_op jit(solution)/shard_map/all_to_all | solution.py:481
  84.8 0.6 select_reduce_fusion
  85.5 9.5 %all-to-all-done = bf16[4,128,128]{1,2,0:T(8,128)(2,1)S(1)} async-done(((bf16[4,128,128]{1,2,0:T(8,128)(2,1)}), bf16[4,128,128]{1,2,0:T(8,128)(2,1)S(1)}, u32[]{:S(2)}, u32[]{:S(2)}) %all-to-all-start) | async-done | bytes 131104 | tf_op jit(solution)/shard_map/all_to_all | solution.py:481
  94.9 5.8 %all-gather.6.cloned.1.call-done = bf16[512,2048]{1,0:T(8,128)(2,1)} async-done(((bf16[32,2048]{1,0:T(8,128)(2,1)}), bf16[512,2048]{1,0:T(8,128)(2,1)}) %all-gather.6.cloned.1.call-update) | async-done | bytes 2097168 | tf_op jit(solution)/shard_map/all_gather | solution.py:392
  100.8 2.2 multiply_reduce_fusion
  103.0 1.0 copy-done.1
  104.1 0.9 multiply_convert_fusion.1.x_ref
  105.0 56.6 %gather_rows.1 = (bf16[16,128,2048]{2,1,0:T(8,128)(2,1)}, f32[16,16,128]{2,1,0:T(8,128)}) custom-call(bf16[128,2048]{1,0:T(8,128)(2,1)} %multiply_convert_fusion.1.x_ref, f32[16,128]{1,0:T(8,128)} %bitcast.100), custom_call_target="tpu_custom_call" | custom-call | tf_op jit(solution)/shard_map/gather_rows/pallas_call | solution.py:342
  161.7 9.8 %fusion.1 = f32[2048,768]{1,0:T(8,128)S(1)} fusion(bf16[2048,2048]{1,0:T(8,128)(2,1)} %bitcast.102, bf16[1,2048,768]{2,1,0:T(8,128)(2,1)S(1)} %copy-done), kind=kOutput, calls=%fused_computation.3 | convolution fusion | flops 6442450944 | bytes 17825792 | tf_op jit(solution)/shard_map/dot_general | solution.py:408
  171.5 8.5 %multiply_convert_fusion = bf16[2048,768]{1,0:T(8,128)(2,1)} fusion(f32[2048,768]{1,0:T(8,128)S(1)} %fusion.1, bf16[2048,2048]{1,0:T(8,128)(2,1)S(1)} %bitcast.103, bf16[1,2048,768]{2,1,0:T(8,128)(2,1)S(1)} %copy-done.9), kind=kOutput, calls=%fused_computation.1 | convolution fusion | flops 6451888128 | bytes 20971520 | tf_op jit(solution)/shard_map/dot_general | solution.py:409
  180.1 0.8 constant_dynamic-slice_fusion
  180.9 1.3 broadcast_in_dim.61.weight_ref
  182.2 58.8 %scatter_sums.1 = f32[128,2048]{1,0:T(8,128)} custom-call(bf16[16,128,768]{2,1,0:T(8,128)(2,1)} %bitcast.85, bf16[768,2048]{1,0:T(8,128)(2,1)} %bitcast.84, f32[16,128,128]{2,1,0:T(8,128)} %broadcast_in_dim.61.weight_ref), custom_call_target="tpu_custom_call" | custom-call | tf_op jit(solution)/shard_map/scatter_sums/pallas_call | solution.py:367
  241.1 2.5 add_convert_fusion
  (32 shorter events, 0.8 us)
Async XLA Ops:
  6.5 155.1 %copy-start = (bf16[1,2048,768]{2,1,0:T(8,128)(2,1)S(1)}, bf16[1,2048,768]{2,1,0:T(8,128)(2,1)}, u32[]{:S(2)}) copy-start(bf16[1,2048,768]{2,1,0:T(8,128)(2,1)} %param.17) | copy-start | bytes 9437188
  6.5 50.8 %all-gather.4.cloned.1.call-start = ((), (), s32[]{:S(2)}) async-start(), calls=%async_computation.1 | async-start | bytes 2621440 | tf_op jit(solution)/shard_map/all_gather | solution.py:426
  7.3 93.5 %all-gather.6.cloned.1.call-start = ((), (), s32[]{:S(2)}) async-start(), calls=%async_computation.2 | async-start | bytes 2228224 | tf_op jit(solution)/shard_map/all_gather | solution.py:392
  60.4 0.8 copy-start.4
  60.4 11.6 %copy-start.5 = (f32[1,128,128]{2,1,0:T(8,128)S(1)}, f32[1,128,128]{2,1,0:T(8,128)}, u32[]{:S(2)}) copy-start(f32[1,128,128]{2,1,0:T(8,128)} %param.13) | copy-start | bytes 196612
  61.3 4.1 %copy-start.2 = (bf16[512,1,1,128]{3,0,2,1:T(8,128)(2,1)}, bf16[512,1,1,128]{3,0,2,1:T(8,128)(2,1)S(1)}, u32[]{:S(2)}) copy-start(bf16[512,1,1,128]{3,0,2,1:T(8,128)(2,1)S(1)} %copy.34) | copy-start | bytes 393220
  63.1 13.2 %collective-permute-start = (bf16[2,1,512,128]{3,2,1,0:T(8,128)(2,1)}, bf16[2,1,512,128]{3,2,1,0:T(8,128)(2,1)}, u32[]{:S(2)}, u32[]{:S(2)}) collective-permute-start(bf16[2,1,512,128]{3,2,1,0:T(8,128)(2,1)} %pad_maximum_fusion), channel_id=1, source_target_pairs={{0,4},{4,8},{8,12},{1,5},{5,9},{9,13},{2,6},{6,10},{10,14},{3,7},{... | collective-permute-start | bytes 786440 | tf_op jit(solution)/shard_map/ppermute | solution.py:29
  72.0 5.4 %copy-start.3 = (bf16[512,1,1,128]{3,0,2,1:T(8,128)(2,1)S(1)}, bf16[512,1,1,128]{3,0,2,1:T(8,128)(2,1)}, u32[]{:S(2)}) copy-start(bf16[512,1,1,128]{3,0,2,1:T(8,128)(2,1)} %copy-done.2) | copy-start | bytes 393220
  78.9 1.0 copy-start.10
  79.9 5.0 %copy-start.6 = (f32[128,8]{0,1:T(8,128)S(1)}, f32[128,8]{0,1:T(8,128)}, u32[]{:S(2)}) copy-start(f32[128,8]{0,1:T(8,128)} %param.21) | copy-start | bytes 12292
  79.9 5.0 %copy-start.7 = (s32[128,8]{0,1:T(8,128)S(1)}, s32[128,8]{0,1:T(8,128)}, u32[]{:S(2)}) copy-start(s32[128,8]{0,1:T(8,128)} %param.20) | copy-start | bytes 12292
  81.2 13.7 %all-to-all-start = ((bf16[4,128,128]{1,2,0:T(8,128)(2,1)}), bf16[4,128,128]{1,2,0:T(8,128)(2,1)S(1)}, u32[]{:S(2)}, u32[]{:S(2)}) async-start(bf16[4,128,128]{1,2,0:T(8,128)(2,1)} %copy.33), calls=%async_computation | async-start | bytes 262144 | tf_op jit(solution)/shard_map/all_to_all | solution.py:481
  103.0 1.1 copy-start.1
  161.6 9.9 %copy-start.8 = (bf16[16,128,2048]{2,1,0:T(8,128)(2,1)S(1)}, bf16[16,128,2048]{2,1,0:T(8,128)(2,1)}, u32[]{:S(2)}) copy-start(bf16[16,128,2048]{2,1,0:T(8,128)(2,1)} %get-tuple-element.61) | copy-start | bytes 25165828
  161.6 9.9 %copy-start.9 = (bf16[1,2048,768]{2,1,0:T(8,128)(2,1)S(1)}, bf16[1,2048,768]{2,1,0:T(8,128)(2,1)}, u32[]{:S(2)}) copy-start(bf16[1,2048,768]{2,1,0:T(8,128)(2,1)} %param.18) | copy-start | bytes 9437188
Sparse Core Ops, SparseCore 0:
  8.9 48.3 all-gather.3
  59.5 41.2 all-gather.5

commit v5 on v4

--- a/solution.py
+++ b/solution.py
@@ -69,28 +69,39 @@
     pl.semaphore_wait(barrier, 2 + jnp.minimum(z, 1) + jnp.minimum(count - 1 - z, 1))
 
 
-def gather_kernel(
-    count, x_ref, t_ref, rows_ref, table_ref, send_x, send_t, recv_x, recv_t, own_sem
-):
+def gather_kernel(count, kinds, *refs):
+    size = len(kinds)
+    groups = [refs[first * size : (first + 1) * size] for first in range(4)]
+    own_sem = refs[4 * size]
     z, c, beside, across, diagonal = place(count)
     greet(z, count, beside, across)
 
+    def origin(kind, source, full):
+        if kind != "share":
+            return source
+        share = full.shape[1]
+        return source.at[pl.ds(pl.multiple_of(c * share, share), share), :]
+
+    def slot_of(kind, zz, cc):
+        return {"group": cc * count + zz, "share": zz * 4 + cc, "line": zz}[kind]
+
     def copies(zz, cc, way, target, own=False):
-        slot = cc * count + zz
-        return [
-            pltpu.make_async_remote_copy(
-                src_ref=source if own else full.at[slot],
-                dst_ref=full.at[slot],
-                send_sem=send.at[way, slot],
-                recv_sem=recv.at[slot],
-                device_id=target,
-                device_id_type=MESH,
+        result = []
+        for kind, source, full, send, recv in zip(kinds, *groups):
+            if kind == "line" and (way > 1 or cc is not c):
+                continue
+            slot = slot_of(kind, zz, cc)
+            result.append(
+                pltpu.make_async_remote_copy(
+                    src_ref=origin(kind, source, full) if own else full.at[slot],
+                    dst_ref=full.at[slot],
+                    send_sem=send.at[way, slot],
+                    recv_sem=recv.at[slot],
+                    device_id=target,
+                    device_id_type=MESH,
+                )
             )
-            for source, full, send, recv in (
-                (x_ref, rows_ref, send_x, recv_x),
-                (t_ref, table_ref, send_t, recv_t),
-            )
-        ]
+        return result
 
     def start(zz, cc, way, target, own=False):
         for copy in copies(zz, cc, way, target, own):
@@ -120,10 +131,11 @@
         act(zz, c, 2, {"ctx": across}, **options)
         act(zz, c, 3, {"ctx": beside}, **options)
 
-    mine = c * count + z
     local = [
-        pltpu.make_async_copy(x_ref, rows_ref.at[mine], own_sem.at[0]),
-        pltpu.make_async_copy(t_ref, table_ref.at[mine], own_sem.at[1]),
+        pltpu.make_async_copy(
+            origin(kind, source, full), full.at[slot_of(kind, z, c)], own_sem.at[index]
+        )
+        for index, (kind, source, full) in enumerate(zip(kinds, *groups[:2]))
     ]
     for copy in local:
         copy.start()
@@ -337,26 +349,29 @@
             down_copy(zz).wait_send()
 
 
-def gather_rows(normed, table):
-    count, devices = lax.axis_size("heads"), lax.axis_size("heads") * lax.axis_size("ctx")
+def gather_blocks(kinds, operands, collective_id, name):
+    count, ctx_count = lax.axis_size("heads"), lax.axis_size("ctx")
+    slots = [count if kind == "line" else count * ctx_count for kind in kinds]
+    shapes = [
+        (value.shape[0] // ctx_count if kind == "share" else value.shape[0], value.shape[1])
+        for kind, value in zip(kinds, operands)
+    ]
     return pl.pallas_call(
-        functools.partial(gather_kernel, count),
+        functools.partial(gather_kernel, count, kinds),
         out_shape=[
-            jax.ShapeDtypeStruct((devices,) + value.shape, value.dtype)
-            for value in (normed, table)
+            jax.ShapeDtypeStruct((slot,) + shape, value.dtype)
+            for slot, shape, value in zip(slots, shapes, operands)
         ],
-        in_specs=[pl.BlockSpec(memory_space=pltpu.VMEM)] * 2,
-        out_specs=[pl.BlockSpec(memory_space=pl.ANY)] * 2,
-        scratch_shapes=[
-            pltpu.SemaphoreType.DMA((4, devices)),
-            pltpu.SemaphoreType.DMA((4, devices)),
-            pltpu.SemaphoreType.DMA((devices,)),
-            pltpu.SemaphoreType.DMA((devices,)),
-            pltpu.SemaphoreType.DMA((2,)),
-        ],
-        compiler_params=pltpu.CompilerParams(collective_id=0, has_side_effects=True),
-        name="gather_rows",
-    )(normed, table)
+        in_specs=[pl.BlockSpec(memory_space=pltpu.VMEM)] * len(kinds),
+        out_specs=[pl.BlockSpec(memory_space=pl.ANY)] * len(kinds),
+        scratch_shapes=[pltpu.SemaphoreType.DMA((4, slot)) for slot in slots]
+        + [pltpu.SemaphoreType.DMA((slot,)) for slot in slots]
+        + [pltpu.SemaphoreType.DMA((len(kinds),))],
+        compiler_params=pltpu.CompilerParams(
+            collective_id=collective_id, has_side_effects=True
+        ),
+        name=name,
+    )(*operands)
 
 
 def scatter_sums(hid, down, weights):
@@ -383,13 +398,12 @@
     )(hid, down, weights)
 
 
-def whole_rows(w_out):
-    ctx_count, rows = lax.axis_size("ctx"), w_out.shape[0]
-    share = rows // ctx_count
-    if rows % ctx_count or share % 16:
-        return lax.all_gather(w_out, "heads", axis=0, tiled=True)
-    mine = lax.dynamic_slice_in_dim(w_out, lax.axis_index("ctx") * share, share, 0)
-    return lax.all_gather(mine, ("heads", "ctx"), axis=0, tiled=True)
+def gather_inputs(tokens, w_out):
+    if lax.axis_size("ctx") == 4 and w_out.shape[0] % 64 == 0:
+        slab, w_rows = gather_blocks(("line", "share"), (tokens, w_out), 2, "gather_inputs")
+        width = tokens.shape[1]
+        return slab.reshape(-1, width), w_rows.reshape(-1, w_out.shape[1])
+    return [lax.all_gather(value, "heads", axis=0, tiled=True) for value in (tokens, w_out)]
 
 
 def dense_experts(
@@ -400,7 +414,9 @@
     chosen = expert_ids[:, :, None] == jnp.arange(expert_count, dtype=jnp.int32)
     table = jnp.sum(jnp.where(chosen, gate_weights[:, :, None], 0.0), axis=1)
     first = lax.axis_index(axes) * exp_local
-    rows, tables = gather_rows(normed, table.T)
+    rows, tables = gather_blocks(
+        ("group", "group"), (normed, table.T), 0, "gather_rows"
+    )
     device_count, row_count, width = rows.shape
     rows = rows.reshape(device_count * row_count, width)
     routed = 0.0
@@ -422,8 +438,9 @@
     inner_width = w_qkv.shape[2]
     local_heads = inner_width // HDIM
     w_flat = w_qkv.reshape(model_width, 3 * inner_width)
+    slab, w_rows = gather_inputs(tokens, w_out)
     projected = jnp.dot(
-        lax.all_gather(tokens, "heads", axis=0, tiled=True),
+        slab,
         w_flat,
         preferred_element_type=jnp.float32,
     ).astype(jnp.bfloat16)
@@ -481,7 +498,7 @@
     regrouped = lax.all_to_all(heads_out, "heads", split_axis=0, concat_axis=1, tiled=True)
     attn = jnp.dot(
         regrouped,
-        whole_rows(w_out),
+        w_rows,
         preferred_element_type=jnp.float32,
     )
     hidden_state = (tokens.astype(jnp.float32) + attn).astype(jnp.bfloat16)

time: 251 us -> 239 us (0.952)
  Pallas kernels: 115 us -> 173 us
  waiting for transfers between devices: 61.6 us -> 5.89 us
  between operations: 13.6 us -> 0.23 us
    pallas_call x1 -> x2, Pallas kernels: 56.6 us -> 111 us  [gather_blocks(): pl.pallas_call(functools.partial(gather_kernel, count, kinds), out_shape=...]
    all_gather x2 -> x0, waiting for transfers between devices: 51.4 us -> none  [the longest x1 45.6 us: on_device(): lax.all_gather(tokens, 'heads', axis=0, tiled=True)]
    all_to_all x1, waiting for transfers between devices: 9.47 us -> 5.89 us  [on_device(): lax.all_to_all(heads_out, 'heads', split_axis=0, concat_axis=1, tiled=True)]
    pallas_call x1, Pallas kernels: 58.8 us -> 61.9 us  [scatter_sums(): pl.pallas_call(functools.partial(scatter_kernel, count), out_shape=jax.Sh...]
  transfers between devices with their start and end apart: 4 -> 2, of which waited for: 3 -> 1; matrix products, arithmetic and copies ran while one was open for 8% -> 3% of each run, Pallas kernels for 0% -> 0%
where the time goes in v5:
time: 239 us; the launch traced here: 238 us
  Pallas kernels  173 us (72%)
  matrix products  31.7 us (13%)
  local copies, waits for them, and re-layouts  9.18 us (4%)
  starting transfers between devices  6.32 us (3%)
  other arithmetic  6.29 us (3%)
  waiting for transfers between devices  5.89 us (2%)
  blocking collectives  5.61 us (2%)
    pallas_call x2, Pallas kernels, gather_blocks(): pl.pallas_call(functools.partial(gather_kernel, count, kinds), out_shape=...  111 us
    pallas_call x1, Pallas kernels, scatter_sums(): pl.pallas_call(functools.partial(scatter_kernel, count), out_shape=jax.Sh...  61.9 us
    dot_general x1, matrix products, dense_experts(): gate_act = jnp.dot(rows, w_gate[e], preferred_element_type=jnp.float32)  9.84 us
    dot_general x1, matrix products, dense_experts(): up_act = jnp.dot(rows, w_up[e], preferred_element_type=jnp.float32)  8.54 us
    all_to_all x1, waiting for transfers between devices, on_device(): lax.all_to_all(heads_out, 'heads', split_axis=0, concat_axis=1, tiled=True)  5.89 us
    all_gather x1, blocking collectives, entering(): gathered = lax.all_gather(x.astype(jnp.bfloat16), axis)  5.61 us
    unnamed x25, local copies, waits for them, and re-layouts  5.56 us
  transfers between devices with their start and end apart: 2, of which 1 were waited for; matrix products, arithmetic and copies ran while one was open for 3% of the time, Pallas kernels for 0%

profile of v5, /device:TPU:0, one launch (start us, length us, event | category | flops | bytes accessed | tf_op | source)
XLA Modules:
  0.0 238.4 jit_solution(9478228116254334570)
XLA Ops:
  0.0 2.8 %copy.27 = bf16[2048,3,128]{0,2,1:T(8,128)(2,1)} copy(bf16[2048,3,128]{2,0,1:T(8,128)(2,1)} %param.15) | data formatting | bytes 3145728 | tf_op args[3]
  2.8 58.6 %gather_inputs.1 = (bf16[4,128,2048]{2,1,0:T(8,128)(2,1)}, bf16[16,32,2048]{2,1,0:T(8,128)(2,1)}) custom-call(bf16[128,2048]{1,0:T(8,128)(2,1)} %refs_0_.1, bf16[128,2048]{1,0:T(8,128)(2,1)} %refs_1_.1), custom_call_target="tpu_custom_call" | custom-call | tf_op jit(solution)/shard_map/gather_inputs/pallas_call | solution.py:359
  61.4 3.0 %convolution_convert_fusion = bf16[512,384]{0,1:T(8,128)(2,1)S(1)} fusion(bf16[512,2048]{1,0:T(8,128)(2,1)} %bitcast.107, bf16[2048,384]{0,1:T(8,128)(2,1)} %bitcast.89), kind=kOutput, calls=%fused_computation.18 | convolution fusion | flops 805502976 | bytes 4063232 | tf_op jit(solution)/shard_map/dot_general | solution.py:442
  64.5 0.7 fusion.34
  65.1 0.1 copy-done.4
  65.2 0.1 copy.34
  65.4 1.1 copy.35
  66.4 0.7 pad_maximum_fusion
  67.2 3.0 %collective-permute-start = (bf16[2,1,512,128]{3,2,1,0:T(8,128)(2,1)}, bf16[2,1,512,128]{3,2,1,0:T(8,128)(2,1)}, u32[]{:S(2)}, u32[]{:S(2)}) collective-permute-start(bf16[2,1,512,128]{3,2,1,0:T(8,128)(2,1)} %pad_maximum_fusion), channel_id=1, source_target_pairs={{0,4},{4,8},{8,12},{1,5},{5,9},{9,13},{2,6},{6,10},{10,14},{3,7},{... | collective-permute-start | bytes 786440 | tf_op jit(solution)/shard_map/ppermute | solution.py:29
  70.2 1.8 convolution_convert_fusion.1
  71.9 5.6 %all-gather = bf16[512,128]{1,0:T(8,128)(2,1)S(1)} all-gather(bf16[128,128]{1,0:T(8,128)(2,1)} %convolution_convert_fusion.1), channel_id=2, replica_groups=mesh['groups'=2,'ctx'=4,'heads'=4] {'ctx'}, dimensions={0}, use_global_device_ids=true | all-gather | bytes 163840 | tf_op jit(solution)/shard_map/all_gather | solution.py:17
  77.6 2.0 fusion.23
  79.5 2.3 multiply_reduce_fusion.1
  81.9 1.1 bitcast_select_fusion
  83.0 1.5 fusion.35
  84.4 0.5 fusion.8
  85.0 0.4 copy-done.10
  85.4 0.6 fusion.12
  86.0 0.8 copy.33
  86.7 3.3 %all-to-all-start = ((bf16[4,128,128]{1,2,0:T(8,128)(2,1)}), bf16[4,128,128]{1,2,0:T(8,128)(2,1)S(1)}, u32[]{:S(2)}, u32[]{:S(2)}) async-start(bf16[4,128,128]{1,2,0:T(8,128)(2,1)} %copy.33), calls=%async_computation | async-start | bytes 262144 | tf_op jit(solution)/shard_map/all_to_all | solution.py:498
  90.1 0.6 select_reduce_fusion
  90.7 5.9 %all-to-all-done = bf16[4,128,128]{1,2,0:T(8,128)(2,1)S(1)} async-done(((bf16[4,128,128]{1,2,0:T(8,128)(2,1)}), bf16[4,128,128]{1,2,0:T(8,128)(2,1)S(1)}, u32[]{:S(2)}, u32[]{:S(2)}) %all-to-all-start) | async-done | bytes 131104 | tf_op jit(solution)/shard_map/all_to_all | solution.py:498
  96.6 2.2 multiply_reduce_fusion
  98.8 1.0 copy-done.1
  99.9 0.9 multiply_convert_fusion.1.refs_0_
  100.8 52.7 %gather_rows.1 = (bf16[16,128,2048]{2,1,0:T(8,128)(2,1)}, f32[16,16,128]{2,1,0:T(8,128)}) custom-call(bf16[128,2048]{1,0:T(8,128)(2,1)} %multiply_convert_fusion.1.refs_0_, f32[16,128]{1,0:T(8,128)} %bitcast.103), custom_call_target="tpu_custom_call" | custom-call | tf_op jit(solution)/shard_map/gather_rows/pallas_call | solution.py:359
  153.5 9.8 %fusion.1 = f32[2048,768]{1,0:T(8,128)S(1)} fusion(bf16[2048,2048]{1,0:T(8,128)(2,1)} %bitcast.105, bf16[1,2048,768]{2,1,0:T(8,128)(2,1)S(1)} %copy-done), kind=kOutput, calls=%fused_computation.3 | convolution fusion | flops 6442450944 | bytes 17825792 | tf_op jit(solution)/shard_map/dot_general | solution.py:424
  163.4 8.5 %multiply_convert_fusion = bf16[2048,768]{1,0:T(8,128)(2,1)} fusion(f32[2048,768]{1,0:T(8,128)S(1)} %fusion.1, bf16[2048,2048]{1,0:T(8,128)(2,1)S(1)} %bitcast.106, bf16[1,2048,768]{2,1,0:T(8,128)(2,1)S(1)} %copy-done.9), kind=kOutput, calls=%fused_computation.1 | convolution fusion | flops 6451888128 | bytes 20971520 | tf_op jit(solution)/shard_map/dot_general | solution.py:425
  171.9 0.8 constant_dynamic-slice_fusion
  172.7 1.3 broadcast_in_dim.61.weight_ref
  174.1 61.9 %scatter_sums.1 = f32[128,2048]{1,0:T(8,128)} custom-call(bf16[16,128,768]{2,1,0:T(8,128)(2,1)} %bitcast.87, bf16[768,2048]{1,0:T(8,128)(2,1)} %bitcast.86, f32[16,128,128]{2,1,0:T(8,128)} %broadcast_in_dim.61.weight_ref), custom_call_target="tpu_custom_call" | custom-call | tf_op jit(solution)/shard_map/scatter_sums/pallas_call | solution.py:382
  235.9 2.5 %add_convert_fusion = bf16[128,2048]{1,0:T(8,128)(2,1)} fusion(f32[128,2048]{1,0:T(8,128)} %copy-done.1, f32[128,2048]{1,0:T(8,128)} %scatter_sums.1), kind=kLoop, calls=%fused_computation.24 | loop fusion | flops 524288 | bytes 2621440 | tf_op jit(solution)/shard_map/convert_element_type | solution.py:431
  (26 shorter events, 0.1 us)
Async XLA Ops:
  0.0 153.5 %copy-start = (bf16[1,2048,768]{2,1,0:T(8,128)(2,1)S(1)}, bf16[1,2048,768]{2,1,0:T(8,128)(2,1)}, u32[]{:S(2)}) copy-start(bf16[1,2048,768]{2,1,0:T(8,128)(2,1)} %param.17) | copy-start | bytes 9437188
  64.4 0.8 copy-start.4
  64.5 13.1 %copy-start.5 = (f32[1,128,128]{2,1,0:T(8,128)S(1)}, f32[1,128,128]{2,1,0:T(8,128)}, u32[]{:S(2)}) copy-start(f32[1,128,128]{2,1,0:T(8,128)} %param.13) | copy-start | bytes 196612
  65.4 6.6 %copy-start.2 = (bf16[512,1,1,128]{3,0,2,1:T(8,128)(2,1)}, bf16[512,1,1,128]{3,0,2,1:T(8,128)(2,1)S(1)}, u32[]{:S(2)}) copy-start(bf16[512,1,1,128]{3,0,2,1:T(8,128)(2,1)S(1)} %copy.34) | copy-start | bytes 393220
  67.2 14.7 %collective-permute-start = (bf16[2,1,512,128]{3,2,1,0:T(8,128)(2,1)}, bf16[2,1,512,128]{3,2,1,0:T(8,128)(2,1)}, u32[]{:S(2)}, u32[]{:S(2)}) collective-permute-start(bf16[2,1,512,128]{3,2,1,0:T(8,128)(2,1)} %pad_maximum_fusion), channel_id=1, source_target_pairs={{0,4},{4,8},{8,12},{1,5},{5,9},{9,13},{2,6},{6,10},{10,14},{3,7},{... | collective-permute-start | bytes 786440 | tf_op jit(solution)/shard_map/ppermute | solution.py:29
  77.6 5.4 %copy-start.3 = (bf16[512,1,1,128]{3,0,2,1:T(8,128)(2,1)S(1)}, bf16[512,1,1,128]{3,0,2,1:T(8,128)(2,1)}, u32[]{:S(2)}) copy-start(bf16[512,1,1,128]{3,0,2,1:T(8,128)(2,1)} %copy-done.2) | copy-start | bytes 393220
  84.4 1.0 copy-start.10
  85.4 4.7 %copy-start.6 = (f32[128,8]{0,1:T(8,128)S(1)}, f32[128,8]{0,1:T(8,128)}, u32[]{:S(2)}) copy-start(f32[128,8]{0,1:T(8,128)} %param.21) | copy-start | bytes 12292
  85.4 4.7 %copy-start.7 = (s32[128,8]{0,1:T(8,128)S(1)}, s32[128,8]{0,1:T(8,128)}, u32[]{:S(2)}) copy-start(s32[128,8]{0,1:T(8,128)} %param.20) | copy-start | bytes 12292
  86.7 9.9 %all-to-all-start = ((bf16[4,128,128]{1,2,0:T(8,128)(2,1)}), bf16[4,128,128]{1,2,0:T(8,128)(2,1)S(1)}, u32[]{:S(2)}, u32[]{:S(2)}) async-start(bf16[4,128,128]{1,2,0:T(8,128)(2,1)} %copy.33), calls=%async_computation | async-start | bytes 262144 | tf_op jit(solution)/shard_map/all_to_all | solution.py:498
  98.8 1.1 copy-start.1
  153.5 9.9 %copy-start.8 = (bf16[16,128,2048]{2,1,0:T(8,128)(2,1)S(1)}, bf16[16,128,2048]{2,1,0:T(8,128)(2,1)}, u32[]{:S(2)}) copy-start(bf16[16,128,2048]{2,1,0:T(8,128)(2,1)} %get-tuple-element.65) | copy-start | bytes 25165828
  153.5 9.9 %copy-start.9 = (bf16[1,2048,768]{2,1,0:T(8,128)(2,1)S(1)}, bf16[1,2048,768]{2,1,0:T(8,128)(2,1)}, u32[]{:S(2)}) copy-start(bf16[1,2048,768]{2,1,0:T(8,128)(2,1)} %param.18) | copy-start | bytes 9437188

commit v6 on v5

--- a/solution.py
+++ b/solution.py
@@ -363,12 +363,12 @@
             for slot, shape, value in zip(slots, shapes, operands)
         ],
         in_specs=[pl.BlockSpec(memory_space=pltpu.VMEM)] * len(kinds),
-        out_specs=[pl.BlockSpec(memory_space=pl.ANY)] * len(kinds),
+        out_specs=[pl.BlockSpec(memory_space=pltpu.VMEM)] * len(kinds),
         scratch_shapes=[pltpu.SemaphoreType.DMA((4, slot)) for slot in slots]
         + [pltpu.SemaphoreType.DMA((slot,)) for slot in slots]
         + [pltpu.SemaphoreType.DMA((len(kinds),))],
         compiler_params=pltpu.CompilerParams(
-            collective_id=collective_id, has_side_effects=True
+            collective_id=collective_id, has_side_effects=True, vmem_limit_bytes=VMEM_BYTES
         ),
         name=name,
     )(*operands)

time: 239 us -> 242 us (1.013)
  Pallas kernels: 173 us -> 176 us
    pallas_call x2, Pallas kernels: 111 us -> 115 us  [gather_blocks(): pl.pallas_call(functools.partial(gather_kernel, count, kinds), out_shape=...]
where the time goes in v6:
time: 242 us; the launch traced here: 241 us
  Pallas kernels  176 us (73%)
  matrix products  31.7 us (13%)
  local copies, waits for them, and re-layouts  9.18 us (4%)
  starting transfers between devices  6.32 us (3%)
  other arithmetic  6.29 us (3%)
  waiting for transfers between devices  5.9 us (2%)
  blocking collectives  5.61 us (2%)
    pallas_call x2, Pallas kernels, gather_blocks(): pl.pallas_call(functools.partial(gather_kernel, count, kinds), out_shape=...  115 us
    pallas_call x1, Pallas kernels, scatter_sums(): pl.pallas_call(functools.partial(scatter_kernel, count), out_shape=jax.Sh...  61.2 us
    dot_general x1, matrix products, dense_experts(): gate_act = jnp.dot(rows, w_gate[e], preferred_element_type=jnp.float32)  9.83 us
    dot_general x1, matrix products, dense_experts(): up_act = jnp.dot(rows, w_up[e], preferred_element_type=jnp.float32)  8.54 us
    all_to_all x1, waiting for transfers between devices, on_device(): lax.all_to_all(heads_out, 'heads', split_axis=0, concat_axis=1, tiled=True)  5.9 us
    all_gather x1, blocking collectives, entering(): gathered = lax.all_gather(x.astype(jnp.bfloat16), axis)  5.61 us
    unnamed x25, local copies, waits for them, and re-layouts  5.56 us
  transfers between devices with their start and end apart: 2, of which 1 were waited for; matrix products, arithmetic and copies ran while one was open for 3% of the time, Pallas kernels for 0%

profile of v6, /device:TPU:0, one launch (start us, length us, event | category | flops | bytes accessed | tf_op | source)
XLA Modules:
  0.0 241.1 jit_solution(4940288365126407644)
XLA Ops:
  0.0 2.8 %copy.27 = bf16[2048,3,128]{0,2,1:T(8,128)(2,1)} copy(bf16[2048,3,128]{2,0,1:T(8,128)(2,1)} %param.15) | data formatting | bytes 3145728 | tf_op args[3]
  2.8 59.4 %gather_inputs.1 = (bf16[4,128,2048]{2,1,0:T(8,128)(2,1)}, bf16[16,32,2048]{2,1,0:T(8,128)(2,1)}) custom-call(bf16[128,2048]{1,0:T(8,128)(2,1)} %refs_0_.1, bf16[128,2048]{1,0:T(8,128)(2,1)} %refs_1_.1), custom_call_target="tpu_custom_call" | custom-call | tf_op jit(solution)/shard_map/gather_inputs/pallas_call | solution.py:359
  62.2 3.0 %convolution_convert_fusion = bf16[512,384]{0,1:T(8,128)(2,1)S(1)} fusion(bf16[512,2048]{1,0:T(8,128)(2,1)} %bitcast.107, bf16[2048,384]{0,1:T(8,128)(2,1)} %bitcast.89), kind=kOutput, calls=%fused_computation.18 | convolution fusion | flops 805502976 | bytes 4063232 | tf_op jit(solution)/shard_map/dot_general | solution.py:442
  65.3 0.7 fusion.34
  65.9 0.1 copy-done.4
  66.0 0.1 copy.34
  66.2 1.1 copy.35
  67.2 0.7 pad_maximum_fusion
  68.0 3.0 %collective-permute-start = (bf16[2,1,512,128]{3,2,1,0:T(8,128)(2,1)}, bf16[2,1,512,128]{3,2,1,0:T(8,128)(2,1)}, u32[]{:S(2)}, u32[]{:S(2)}) collective-permute-start(bf16[2,1,512,128]{3,2,1,0:T(8,128)(2,1)} %pad_maximum_fusion), channel_id=1, source_target_pairs={{0,4},{4,8},{8,12},{1,5},{5,9},{9,13},{2,6},{6,10},{10,14},{3,7},{... | collective-permute-start | bytes 786440 | tf_op jit(solution)/shard_map/ppermute | solution.py:29
  71.0 1.8 convolution_convert_fusion.1
  72.7 5.6 %all-gather = bf16[512,128]{1,0:T(8,128)(2,1)S(1)} all-gather(bf16[128,128]{1,0:T(8,128)(2,1)} %convolution_convert_fusion.1), channel_id=2, replica_groups=mesh['groups'=2,'ctx'=4,'heads'=4] {'ctx'}, dimensions={0}, use_global_device_ids=true | all-gather | bytes 163840 | tf_op jit(solution)/shard_map/all_gather | solution.py:17
  78.4 2.0 fusion.23
  80.3 2.3 multiply_reduce_fusion.1
  82.7 1.1 bitcast_select_fusion
  83.8 1.5 fusion.35
  85.2 0.5 fusion.8
  85.7 0.4 copy-done.10
  86.2 0.6 fusion.12
  86.8 0.8 copy.33
  87.5 3.3 %all-to-all-start = ((bf16[4,128,128]{1,2,0:T(8,128)(2,1)}), bf16[4,128,128]{1,2,0:T(8,128)(2,1)S(1)}, u32[]{:S(2)}, u32[]{:S(2)}) async-start(bf16[4,128,128]{1,2,0:T(8,128)(2,1)} %copy.33), calls=%async_computation | async-start | bytes 262144 | tf_op jit(solution)/shard_map/all_to_all | solution.py:498
  90.9 0.6 select_reduce_fusion
  91.5 5.9 %all-to-all-done = bf16[4,128,128]{1,2,0:T(8,128)(2,1)S(1)} async-done(((bf16[4,128,128]{1,2,0:T(8,128)(2,1)}), bf16[4,128,128]{1,2,0:T(8,128)(2,1)S(1)}, u32[]{:S(2)}, u32[]{:S(2)}) %all-to-all-start) | async-done | bytes 131104 | tf_op jit(solution)/shard_map/all_to_all | solution.py:498
  97.4 2.2 multiply_reduce_fusion
  99.6 1.0 copy-done.1
  100.7 0.9 multiply_convert_fusion.1.refs_0_
  101.6 55.3 %gather_rows.1 = (bf16[16,128,2048]{2,1,0:T(8,128)(2,1)}, f32[16,16,128]{2,1,0:T(8,128)}) custom-call(bf16[128,2048]{1,0:T(8,128)(2,1)} %multiply_convert_fusion.1.refs_0_, f32[16,128]{1,0:T(8,128)} %bitcast.103), custom_call_target="tpu_custom_call" | custom-call | tf_op jit(solution)/shard_map/gather_rows/pallas_call | solution.py:359
  156.9 9.8 %fusion.1 = f32[2048,768]{1,0:T(8,128)S(1)} fusion(bf16[2048,2048]{1,0:T(8,128)(2,1)} %bitcast.105, bf16[1,2048,768]{2,1,0:T(8,128)(2,1)S(1)} %copy-done), kind=kOutput, calls=%fused_computation.3 | convolution fusion | flops 6442450944 | bytes 17825792 | tf_op jit(solution)/shard_map/dot_general | solution.py:424
  166.7 8.5 %multiply_convert_fusion = bf16[2048,768]{1,0:T(8,128)(2,1)} fusion(f32[2048,768]{1,0:T(8,128)S(1)} %fusion.1, bf16[2048,2048]{1,0:T(8,128)(2,1)S(1)} %bitcast.106, bf16[1,2048,768]{2,1,0:T(8,128)(2,1)S(1)} %copy-done.9), kind=kOutput, calls=%fused_computation.1 | convolution fusion | flops 6451888128 | bytes 20971520 | tf_op jit(solution)/shard_map/dot_general | solution.py:425
  175.3 0.8 constant_dynamic-slice_fusion
  176.1 1.3 broadcast_in_dim.61.weight_ref
  177.4 61.2 %scatter_sums.1 = f32[128,2048]{1,0:T(8,128)} custom-call(bf16[16,128,768]{2,1,0:T(8,128)(2,1)} %bitcast.87, bf16[768,2048]{1,0:T(8,128)(2,1)} %bitcast.86, f32[16,128,128]{2,1,0:T(8,128)} %broadcast_in_dim.61.weight_ref), custom_call_target="tpu_custom_call" | custom-call | tf_op jit(solution)/shard_map/scatter_sums/pallas_call | solution.py:382
  238.6 2.5 %add_convert_fusion = bf16[128,2048]{1,0:T(8,128)(2,1)} fusion(f32[128,2048]{1,0:T(8,128)} %copy-done.1, f32[128,2048]{1,0:T(8,128)} %scatter_sums.1), kind=kLoop, calls=%fused_computation.24 | loop fusion | flops 524288 | bytes 2621440 | tf_op jit(solution)/shard_map/convert_element_type | solution.py:431
  (26 shorter events, 0.1 us)
Async XLA Ops:
  0.0 156.9 %copy-start = (bf16[1,2048,768]{2,1,0:T(8,128)(2,1)S(1)}, bf16[1,2048,768]{2,1,0:T(8,128)(2,1)}, u32[]{:S(2)}) copy-start(bf16[1,2048,768]{2,1,0:T(8,128)(2,1)} %param.17) | copy-start | bytes 9437188
  65.2 0.8 copy-start.4
  65.3 13.1 %copy-start.5 = (f32[1,128,128]{2,1,0:T(8,128)S(1)}, f32[1,128,128]{2,1,0:T(8,128)}, u32[]{:S(2)}) copy-start(f32[1,128,128]{2,1,0:T(8,128)} %param.13) | copy-start | bytes 196612
  66.2 6.6 %copy-start.2 = (bf16[512,1,1,128]{3,0,2,1:T(8,128)(2,1)}, bf16[512,1,1,128]{3,0,2,1:T(8,128)(2,1)S(1)}, u32[]{:S(2)}) copy-start(bf16[512,1,1,128]{3,0,2,1:T(8,128)(2,1)S(1)} %copy.34) | copy-start | bytes 393220
  68.0 14.7 %collective-permute-start = (bf16[2,1,512,128]{3,2,1,0:T(8,128)(2,1)}, bf16[2,1,512,128]{3,2,1,0:T(8,128)(2,1)}, u32[]{:S(2)}, u32[]{:S(2)}) collective-permute-start(bf16[2,1,512,128]{3,2,1,0:T(8,128)(2,1)} %pad_maximum_fusion), channel_id=1, source_target_pairs={{0,4},{4,8},{8,12},{1,5},{5,9},{9,13},{2,6},{6,10},{10,14},{3,7},{... | collective-permute-start | bytes 786440 | tf_op jit(solution)/shard_map/ppermute | solution.py:29
  78.4 5.4 %copy-start.3 = (bf16[512,1,1,128]{3,0,2,1:T(8,128)(2,1)S(1)}, bf16[512,1,1,128]{3,0,2,1:T(8,128)(2,1)}, u32[]{:S(2)}) copy-start(bf16[512,1,1,128]{3,0,2,1:T(8,128)(2,1)} %copy-done.2) | copy-start | bytes 393220
  85.2 1.0 copy-start.10
  86.2 4.7 %copy-start.6 = (f32[128,8]{0,1:T(8,128)S(1)}, f32[128,8]{0,1:T(8,128)}, u32[]{:S(2)}) copy-start(f32[128,8]{0,1:T(8,128)} %param.21) | copy-start | bytes 12292
  86.2 4.7 %copy-start.7 = (s32[128,8]{0,1:T(8,128)S(1)}, s32[128,8]{0,1:T(8,128)}, u32[]{:S(2)}) copy-start(s32[128,8]{0,1:T(8,128)} %param.20) | copy-start | bytes 12292
  87.5 9.9 %all-to-all-start = ((bf16[4,128,128]{1,2,0:T(8,128)(2,1)}), bf16[4,128,128]{1,2,0:T(8,128)(2,1)S(1)}, u32[]{:S(2)}, u32[]{:S(2)}) async-start(bf16[4,128,128]{1,2,0:T(8,128)(2,1)} %copy.33), calls=%async_computation | async-start | bytes 262144 | tf_op jit(solution)/shard_map/all_to_all | solution.py:498
  99.6 1.1 copy-start.1
  156.9 9.9 %copy-start.8 = (bf16[16,128,2048]{2,1,0:T(8,128)(2,1)S(1)}, bf16[16,128,2048]{2,1,0:T(8,128)(2,1)}, u32[]{:S(2)}) copy-start(bf16[16,128,2048]{2,1,0:T(8,128)(2,1)} %get-tuple-element.65) | copy-start | bytes 25165828
  156.9 9.9 %copy-start.9 = (bf16[1,2048,768]{2,1,0:T(8,128)(2,1)S(1)}, bf16[1,2048,768]{2,1,0:T(8,128)(2,1)}, u32[]{:S(2)}) copy-start(bf16[1,2048,768]{2,1,0:T(8,128)(2,1)} %param.18) | copy-start | bytes 9437188
